TPU v7x, 256 devices: a whole 4x4x8 slice. The times are simulated.
256 devices in a mesh: segment: 4 (over y), mp: 16 (over z, core), dp: 4 (over x).
Axes of the slice: x: 4, y: 4, z: 8, core: 2. Of those that a mesh axis runs over, the one named last changes fastest.
Arguments:
- text_rows: bfloat16 [4, 512, 1024], P(None, 'dp'), may hold values from -6 to 6
- durations: int32 [4, 4, 128], P(None, 'dp'), may hold values from 1 to 16, 512 in all within a row
- unit_targets: int32 [4, 2048], P(None, 'dp'), may hold values from 0 to 9999
- w_in: bfloat16 [4, 1024, 8192], P('segment', None, 'mp'), may hold values from -0.1875 to 0.1875
- w_out: bfloat16 [4, 8192, 1024], P('segment', 'mp'), may hold values from -0.0625 to 0.0625
- w_unit: bfloat16 [1024, 10240], P(None, ('segment', 'mp')), as said below
Outputs:
- loss: float32 [4], P('dp')
- grad_in: float32 [4, 1024, 8192], P('segment', 'dp', 'mp')
- grad_out: float32 [4, 8192, 1024], P('segment', 'mp', 'dp')
- grad_unit: float32 [1024, 10240], P('dp', ('segment', 'mp'))
Inputs may be any that keep to these rules, and one draw needn't show every extreme that they name: Within each micro-batch and each index of dp the 128 durations sum to exactly 512, and one of them equals 16. `w_unit`: entries of order 3 / sqrt(1024) in most columns, some columns much larger.
All inputs are finite; a program needn't handle non-finite values.
Results may differ from a plain program's by a relative error of at most 0.035.
Values may be sent and summed in bfloat16 or wider, within the bound.
A program may use at most 128 MiB of HBM per device.

v0:
```python
import jax
import jax.numpy as jnp
from jax import lax
from jax.sharding import PartitionSpec as P


def shifted(block, axis, distance):
    devices = range(lax.axis_size(axis))
    route = [(i - distance, i) for i in devices if i - distance in devices]
    return lax.ppermute(block, axis, route)


def broadcast(x, axis, root):
    mine = lax.axis_index(axis) == root
    return lax.psum(jnp.where(mine, x, jnp.zeros_like(x)), axis)


def gelu_parts(pre_vals):
    coeff = 0.7978845608
    inner = coeff * (pre_vals + 0.044715 * pre_vals * pre_vals * pre_vals)
    tanh_val = jnp.tanh(inner)
    value = 0.5 * pre_vals * (1.0 + tanh_val)
    slope = 0.5 * (1.0 + tanh_val) + 0.5 * pre_vals * (1.0 - tanh_val * tanh_val) * coeff * (
        1.0 + 3.0 * 0.044715 * pre_vals * pre_vals
    )
    return (value, slope)


def row_scale(rows_in):
    floats = rows_in.astype(jnp.float32)
    return lax.rsqrt(jnp.mean(floats * floats, axis=-1, keepdims=True) + 1e-06)


def norm_back(rows_in, grads):
    scale = row_scale(rows_in)
    normal = rows_in.astype(jnp.float32) * scale
    return scale * (grads - normal * jnp.mean(grads * normal, axis=-1, keepdims=True))


def section(rows_in, first):
    normed = (rows_in.astype(jnp.float32) * row_scale(rows_in)).astype(jnp.bfloat16)
    pre_vals = jnp.dot(normed, first, preferred_element_type=jnp.float32)
    value, slope = gelu_parts(pre_vals)
    return (normed, value.astype(jnp.bfloat16), slope)


def finish_forward(pieces, summed):
    return (pieces[0].astype(jnp.float32) + summed).astype(jnp.bfloat16)


def finish_backward(pieces, summed):
    return (pieces[0].astype(jnp.float32) + norm_back(pieces[1], summed)).astype(jnp.bfloat16)


def reduce_rows(partial_value, pieces, finisher):
    summed = lax.psum(partial_value, "mp")
    return finisher(pieces, summed)


def on_device(text_rows, durations, unit_targets, w_in, w_out, w_unit):
    micro_count, row_count, width = text_rows.shape
    segments = lax.axis_size("segment")
    segment_at = lax.axis_index("segment")
    first = w_in[0]
    second = w_out[0]
    clocks = micro_count + segments - 1
    stash = jnp.zeros((micro_count, row_count, width), jnp.bfloat16)
    final_rows = jnp.zeros((micro_count, row_count, width), jnp.bfloat16)
    outgoing = jnp.zeros((row_count, width), jnp.bfloat16)
    for clock in range(clocks):
        if clock > 0:
            incoming = shifted(outgoing, "segment", 1)
        else:
            incoming = jnp.zeros((row_count, width), jnp.bfloat16)
        rows_in = jnp.where(segment_at == 0, text_rows[min(clock, micro_count - 1)], incoming)
        batch_at = clock - segment_at
        is_live = (batch_at >= 0) & (batch_at < micro_count)
        slot_at = jnp.clip(batch_at, 0, micro_count - 1)
        stash = jnp.where(
            is_live, lax.dynamic_update_index_in_dim(stash, rows_in, slot_at, 0), stash
        )
        normed, hidden, slope = section(rows_in, first)
        partial_value = jnp.dot(hidden, second, preferred_element_type=jnp.float32)
        outgoing = reduce_rows(partial_value, (rows_in,), finish_forward)
        is_last = is_live & (segment_at == segments - 1)
        final_rows = jnp.where(
            is_last, lax.dynamic_update_index_in_dim(final_rows, outgoing, slot_at, 0), final_rows
        )
    final_rows = broadcast(final_rows, "segment", segments - 1)
    vocab_part = w_unit.shape[1]
    vocab_start = lax.axis_index(("segment", "mp")) * vocab_part
    final_norm = (final_rows.astype(jnp.float32) * row_scale(final_rows)).astype(jnp.bfloat16)
    logits = jnp.einsum("mrd,dv->mrv", final_norm, w_unit, preferred_element_type=jnp.float32)
    lengths = durations[:, 0, :]
    unit_count = unit_targets.shape[1]
    ends = jnp.cumsum(lengths, axis=-1)
    positions = jnp.arange(unit_count, dtype=jnp.int32)
    row_local = jnp.sum((ends[:, None, :] <= positions[None, :, None]).astype(jnp.int32), axis=-1)
    row_onehot = (
        row_local[:, :, None] == jnp.arange(row_count, dtype=jnp.int32)[None, None, :]
    ).astype(jnp.bfloat16)
    vocab_ids = vocab_start + jnp.arange(vocab_part, dtype=jnp.int32)
    target_hits = (unit_targets[:, :, None] == vocab_ids[None, None, :]).astype(jnp.bfloat16)
    counts = jnp.einsum("mur,muv->mrv", row_onehot, target_hits, preferred_element_type=jnp.float32)
    local_peak = jnp.max(logits, axis=-1)
    target_local = jnp.sum(counts * logits, axis=-1)
    peak = lax.pmax(local_peak, ("segment", "mp"))
    total, target_sum = lax.psum(
        (jnp.sum(jnp.exp(logits - peak[..., None]), axis=-1), target_local), ("segment", "mp")
    )
    lse = peak + jnp.log(total)
    denom = float(micro_count * unit_count * lax.axis_size("dp"))
    length_f = lengths.astype(jnp.float32)
    loss_local = jnp.sum(length_f * lse - target_sum)
    loss = (loss_local / denom)[None]
    dlogits = ((length_f[..., None] * jnp.exp(logits - lse[..., None]) - counts) / denom).astype(
        jnp.bfloat16
    )
    grad_unit = jnp.einsum("mrd,mrv->dv", final_norm, dlogits, preferred_element_type=jnp.float32)
    norm_part = jnp.einsum("mrv,dv->mrd", dlogits, w_unit, preferred_element_type=jnp.float32)
    norm_share = lax.psum_scatter(
        norm_part, ("segment", "mp"), scatter_dimension=2, tiled=True
    ).astype(jnp.bfloat16)
    dnorm = lax.all_gather(norm_share, ("segment", "mp"), axis=2, tiled=True)
    grad_final = norm_back(final_rows, dnorm.astype(jnp.float32)).astype(jnp.bfloat16)
    grad_first = jnp.zeros(first.shape, jnp.float32)
    grad_second = jnp.zeros(second.shape, jnp.float32)
    going_back = jnp.zeros((row_count, width), jnp.bfloat16)
    for clock in range(clocks):
        if clock > 0:
            arriving = shifted(going_back, "segment", -1)
        else:
            arriving = jnp.zeros((row_count, width), jnp.bfloat16)
        grad_rows = jnp.where(
            segment_at == segments - 1, grad_final[min(clock, micro_count - 1)], arriving
        )
        batch_at = clock - (segments - 1 - segment_at)
        is_live = (batch_at >= 0) & (batch_at < micro_count)
        slot_at = jnp.clip(batch_at, 0, micro_count - 1)
        rows_in = lax.dynamic_index_in_dim(stash, slot_at, 0, keepdims=False)
        normed, hidden, slope = section(rows_in, first)
        live_f = is_live.astype(jnp.float32)
        grad_second = grad_second + live_f * jnp.dot(
            hidden.T, grad_rows, preferred_element_type=jnp.float32
        )
        dhidden = jnp.dot(grad_rows, second.T, preferred_element_type=jnp.float32)
        dpre = (dhidden * slope).astype(jnp.bfloat16)
        grad_first = grad_first + live_f * jnp.dot(
            normed.T, dpre, preferred_element_type=jnp.float32
        )
        dnormed = jnp.dot(dpre, first.T, preferred_element_type=jnp.float32)
        going_back = reduce_rows(dnormed, (grad_rows, rows_in), finish_backward)
    sum_first, sum_second, sum_unit = (
        lax.psum_scatter(grad_first, "dp", scatter_dimension=0, tiled=True),
        lax.psum_scatter(grad_second, "dp", scatter_dimension=1, tiled=True),
        lax.psum_scatter(grad_unit, "dp", scatter_dimension=0, tiled=True),
    )
    return (loss, sum_first[None], sum_second[None], sum_unit)


def solution(mesh):
    placed = (
        P(None, "dp", None),
        P(None, "dp", None),
        P(None, "dp"),
        P("segment", None, "mp"),
        P("segment", "mp", None),
        P(None, ("segment", "mp")),
    )
    return jax.shard_map(
        on_device,
        mesh=mesh,
        in_specs=placed,
        out_specs=(
            P("dp"),
            P("segment", "dp", "mp"),
            P("segment", "mp", "dp"),
            P("dp", ("segment", "mp")),
        ),
        check_vma=False,
    )
```

profile of v0, /device:TPU:1, one launch (start us, length us, event | category | flops | bytes accessed | tf_op | source)
XLA Modules:
  0.0 2379.7 jit_solution(6565013018614124377)
XLA Ops:
  11.3 113.5 %all-reduce.18.cloned.1.call-done = f32[128,1024]{1,0:T(8,128)} async-done(((f32[128,1024]{1,0:T(8,128)}), f32[128,1024]{1,0:T(8,128)}) %all-reduce.18.cloned.1.call-update) | async-done | bytes 524304 | tf_op jit(solution)/shard_map/psum | solution.py:56
  137.0 111.0 %all-reduce.20.cloned.1.call-done = f32[128,1024]{1,0:T(8,128)} async-done(((f32[128,1024]{1,0:T(8,128)}), f32[128,1024]{1,0:T(8,128)}) %all-reduce.20.cloned.1.call-update) | async-done | bytes 524304 | tf_op jit(solution)/shard_map/psum | solution.py:56
  253.2 5.2 collective-permute-done.1
  261.9 110.8 %all-reduce.22.cloned.1.call-done = f32[128,1024]{1,0:T(8,128)} async-done(((f32[128,1024]{1,0:T(8,128)}), f32[128,1024]{1,0:T(8,128)}) %all-reduce.22.cloned.1.call-update) | async-done | bytes 524304 | tf_op jit(solution)/shard_map/psum | solution.py:56
  377.8 5.2 collective-permute-done.2
  386.5 110.8 %all-reduce.24.cloned.1.call-done = f32[128,1024]{1,0:T(8,128)} async-done(((f32[128,1024]{1,0:T(8,128)}), f32[128,1024]{1,0:T(8,128)}) %all-reduce.24.cloned.1.call-update) | async-done | bytes 524304 | tf_op jit(solution)/shard_map/psum | solution.py:56
  502.4 5.2 collective-permute-done.3
  511.1 110.8 %all-reduce.26.cloned.1.call-done = f32[128,1024]{1,0:T(8,128)} async-done(((f32[128,1024]{1,0:T(8,128)}), f32[128,1024]{1,0:T(8,128)}) %all-reduce.26.cloned.1.call-update) | async-done | bytes 524304 | tf_op jit(solution)/shard_map/psum | solution.py:56
  627.0 5.2 collective-permute-done.4
  635.7 110.8 %all-reduce.28.cloned.1.call-done = f32[128,1024]{1,0:T(8,128)} async-done(((f32[128,1024]{1,0:T(8,128)}), f32[128,1024]{1,0:T(8,128)}) %all-reduce.28.cloned.1.call-update) | async-done | bytes 524304 | tf_op jit(solution)/shard_map/psum | solution.py:56
  760.3 110.8 %all-reduce.30.cloned.1.call-done = f32[128,1024]{1,0:T(8,128)} async-done(((f32[128,1024]{1,0:T(8,128)}), f32[128,1024]{1,0:T(8,128)}) %all-reduce.30.cloned.1.call-update) | async-done | bytes 524304 | tf_op jit(solution)/shard_map/psum | solution.py:56
  876.2 49.1 %all-reduce.32.cloned.1.call-done = bf16[4,128,1024]{2,1,0:T(8,128)(2,1)} async-done(((bf16[4,128,1024]{2,1,0:T(8,128)(2,1)}), bf16[4,128,1024]{2,1,0:T(8,128)(2,1)}) %all-reduce.32.cloned.1.call-update) | async-done | bytes 1048592 | tf_op jit(solution)/shard_map/psum | solution.py:15
  929.3 125.5 %pmax.7 = f32[4,128]{1,0:T(4,128)S(1)} all-reduce(f32[4,128]{1,0:T(4,128)S(1)} %get-tuple-element.40), channel_id=1, replica_groups=mesh['segment'=4,'mp'=16,'dp'=4] {'segment','mp'}, use_global_device_ids=true, to_apply=%region_17.18 | all-reduce | flops 512 | bytes 4096 | tf_op jit(solution)/shard_map/pmax | solution.py:107
  1057.1 127.1 %psum.120 = f32[4,128]{1,0:T(4,128)S(1)} all-reduce(f32[4,128]{1,0:T(4,128)S(1)} %get-tuple-element.12), channel_id=1, replica_groups=mesh['segment'=4,'mp'=16,'dp'=4] {'segment','mp'}, use_global_device_ids=true, to_apply=%region_19.20 | all-reduce | flops 512 | bytes 4096 | tf_op jit(solution)/shard_map/psum | solution.py:108
  1189.2 265.5 %all-reduce.45 = (f32[4,128]{1,0:T(4,128)}, bf16[4,128,1024]{1,0,2:T(4,128)(2,1)}) all-reduce(f32[4,128]{1,0:T(4,128)S(1)} %get-tuple-element.13, f32[4,128,1024]{1,0,2:T(4,128)} %copy.13), channel_id=1, replica_groups=mesh['segment'=4,'mp'=16,'dp'=4] {'segment','mp'}, use_global_device_ids=true, to_apply=%region_23.24 | all-reduce | flops 524800 | bytes 3149824 | tf_op jit(solution)/shard_map/psum | solution.py:108
  1456.9 75.1 %all-gather.2.cloned.1.call-done = bf16[4,128,1024]{1,0,2:T(4,128)(2,1)} async-done(((bf16[4,128,16]{1,0,2:T(4,128)(2,1)}), bf16[4,128,1024]{1,0,2:T(4,128)(2,1)}) %all-gather.2.cloned.1.call-update) | async-done | bytes 1048592 | tf_op jit(solution)/shard_map/all_gather | solution.py:124
  1540.1 106.9 %all-reduce.34.cloned.1.call-done = f32[128,1024]{1,0:T(8,128)} async-done(((f32[128,1024]{1,0:T(8,128)}), f32[128,1024]{1,0:T(8,128)}) %all-reduce.34.cloned.1.call-update) | async-done | bytes 524304 | tf_op jit(solution)/shard_map/psum | solution.py:56
  1651.1 7.3 collective-permute-done.6
  1661.0 109.8 %all-reduce.36.cloned.1.call-done = f32[128,1024]{1,0:T(8,128)} async-done(((f32[128,1024]{1,0:T(8,128)}), f32[128,1024]{1,0:T(8,128)}) %all-reduce.36.cloned.1.call-update) | async-done | bytes 524304 | tf_op jit(solution)/shard_map/psum | solution.py:56
  1775.8 6.7 collective-permute-done.7
  1786.7 109.8 %all-reduce.38.cloned.1.call-done = f32[128,1024]{1,0:T(8,128)} async-done(((f32[128,1024]{1,0:T(8,128)}), f32[128,1024]{1,0:T(8,128)}) %all-reduce.38.cloned.1.call-update) | async-done | bytes 524304 | tf_op jit(solution)/shard_map/psum | solution.py:56
  1901.5 6.7 collective-permute-done.8
  1912.4 109.8 %all-reduce.40.cloned.1.call-done = f32[128,1024]{1,0:T(8,128)} async-done(((f32[128,1024]{1,0:T(8,128)}), f32[128,1024]{1,0:T(8,128)}) %all-reduce.40.cloned.1.call-update) | async-done | bytes 524304 | tf_op jit(solution)/shard_map/psum | solution.py:56
  2027.3 6.7 collective-permute-done.9
  2038.2 109.8 %all-reduce.42.cloned.1.call-done = f32[128,1024]{1,0:T(8,128)} async-done(((f32[128,1024]{1,0:T(8,128)}), f32[128,1024]{1,0:T(8,128)}) %all-reduce.42.cloned.1.call-update) | async-done | bytes 524304 | tf_op jit(solution)/shard_map/psum | solution.py:56
  2153.0 6.7 collective-permute-done.10
  2178.9 94.8 %all-reduce.44.cloned.1.call-done = f32[128,1024]{1,0:T(8,128)} async-done(((f32[128,1024]{1,0:T(8,128)}), f32[128,1024]{1,0:T(8,128)}) %all-reduce.44.cloned.1.call-update) | async-done | bytes 524304 | tf_op jit(solution)/shard_map/psum | solution.py:56
  2278.2 7.3 collective-permute-done.11
  2286.2 6.7 multiply_add_fusion
  2305.0 7.7 multiply_add_fusion.1
  2314.6 21.9 reduce-scatter.6.cloned.1.call-done
  2336.6 35.2 %reduce-scatter.4.cloned.1.call-done = f32[256,512]{1,0:T(8,128)} async-done(((f32[1024,512]{1,0:T(8,128)}), f32[256,512]{1,0:T(8,128)}) %reduce-scatter.4.cloned.1.call-update) | async-done | bytes 524304 | tf_op jit(solution)/shard_map/reduce_scatter | solution.py:154
  (293 shorter events, 166.7 us)
Async XLA Ops:
  7.2 117.6 %all-reduce.18.cloned.1.call-start = ((), (), s32[]{:S(2)}) async-start(), calls=%async_computation.3 | async-start | bytes 1048576 | tf_op jit(solution)/shard_map/psum | solution.py:56
  11.2 236.8 %all-reduce.20.cloned.1.call-start = ((), (), s32[]{:S(2)}) async-start(), calls=%async_computation.4 | async-start | bytes 1048576 | tf_op jit(solution)/shard_map/psum | solution.py:56
  126.2 8.0 collective-permute-start
  137.0 235.7 %all-reduce.22.cloned.1.call-start = ((), (), s32[]{:S(2)}) async-start(), calls=%async_computation.5 | async-start | bytes 1048576 | tf_op jit(solution)/shard_map/psum | solution.py:56
  250.1 8.3 collective-permute-start.1
  261.8 235.4 %all-reduce.24.cloned.1.call-start = ((), (), s32[]{:S(2)}) async-start(), calls=%async_computation.6 | async-start | bytes 1048576 | tf_op jit(solution)/shard_map/psum | solution.py:56
  374.7 8.3 collective-permute-start.2
  386.4 235.4 %all-reduce.26.cloned.1.call-start = ((), (), s32[]{:S(2)}) async-start(), calls=%async_computation.7 | async-start | bytes 1048576 | tf_op jit(solution)/shard_map/psum | solution.py:56
  499.3 8.3 collective-permute-start.3
  511.0 235.4 %all-reduce.28.cloned.1.call-start = ((), (), s32[]{:S(2)}) async-start(), calls=%async_computation.8 | async-start | bytes 1048576 | tf_op jit(solution)/shard_map/psum | solution.py:56
  623.9 8.3 collective-permute-start.4
  635.7 235.4 %all-reduce.30.cloned.1.call-start = ((), (), s32[]{:S(2)}) async-start(), calls=%async_computation.9 | async-start | bytes 1048576 | tf_op jit(solution)/shard_map/psum | solution.py:56
  748.5 8.3 collective-permute-start.5
  760.3 165.0 %all-reduce.32.cloned.1.call-start = ((), (), s32[]{:S(2)}) async-start(), calls=%async_computation.10 | async-start | bytes 2097152 | tf_op jit(solution)/shard_map/psum | solution.py:15
  874.2 180.6 %copy-start.59 = (s32[4,512]{1,0:T(4,128)S(1)}, s32[4,512]{1,0:T(4,128)}, u32[]{:S(2)}) copy-start(s32[4,512]{1,0:T(4,128)} %param.8) | copy-start | bytes 24580
  874.2 657.7 %all-gather.2.cloned.1.call-start = ((), (), s32[]{:S(2)}) async-start(), calls=%async_computation.11 | async-start | bytes 1064960 | tf_op jit(solution)/shard_map/all_gather | solution.py:124
  1456.1 190.9 %all-reduce.34.cloned.1.call-start = ((), (), s32[]{:S(2)}) async-start(), calls=%async_computation.12 | async-start | bytes 1048576 | tf_op jit(solution)/shard_map/psum | solution.py:56
  1456.5 192.7 %copy-start.55 = (f32[128]{0:T(128)}, f32[128]{0:T(128)S(1)}, u32[]{:S(2)}) copy-start(f32[128]{0:T(128)S(1)} %add_rsqrt_fusion.7) | copy-start | bytes 1540
  1540.0 230.8 %all-reduce.36.cloned.1.call-start = ((), (), s32[]{:S(2)}) async-start(), calls=%async_computation.13 | async-start | bytes 1048576 | tf_op jit(solution)/shard_map/psum | solution.py:56
  1649.4 9.0 collective-permute-start.6
  1661.0 235.5 %all-reduce.38.cloned.1.call-start = ((), (), s32[]{:S(2)}) async-start(), calls=%async_computation.14 | async-start | bytes 1048576 | tf_op jit(solution)/shard_map/psum | solution.py:56
  1773.4 9.0 collective-permute-start.7
  1786.6 235.6 %all-reduce.40.cloned.1.call-start = ((), (), s32[]{:S(2)}) async-start(), calls=%async_computation.15 | async-start | bytes 1048576 | tf_op jit(solution)/shard_map/psum | solution.py:56
  1899.1 9.0 collective-permute-start.8
  1912.4 235.6 %all-reduce.42.cloned.1.call-start = ((), (), s32[]{:S(2)}) async-start(), calls=%async_computation.16 | async-start | bytes 1048576 | tf_op jit(solution)/shard_map/psum | solution.py:56
  2024.9 9.0 collective-permute-start.9
  2038.1 235.6 %all-reduce.44.cloned.1.call-start = ((), (), s32[]{:S(2)}) async-start(), calls=%async_computation.17 | async-start | bytes 1048576 | tf_op jit(solution)/shard_map/psum | solution.py:56
  2150.7 9.0 collective-permute-start.10
  2163.9 150.7 %reduce-scatter.8.cloned.1.call-start = ((), (), s32[]{:S(2)}) async-start(), calls=%async_computation.20 | async-start | bytes 819200 | tf_op jit(solution)/shard_map/reduce_scatter | solution.py:156
  2166.6 169.9 %reduce-scatter.6.cloned.1.call-start = ((), (), s32[]{:S(2)}) async-start(), calls=%async_computation.19 | async-start | bytes 2621440 | tf_op jit(solution)/shard_map/reduce_scatter | solution.py:155
  2276.5 9.0 collective-permute-start.11
  2292.9 78.8 %reduce-scatter.4.cloned.1.call-start = ((), (), s32[]{:S(2)}) async-start(), calls=%async_computation.18 | async-start | bytes 2621440 | tf_op jit(solution)/shard_map/reduce_scatter | solution.py:154
  (59 other events, 808.3 us)
Sparse Core Ops, SparseCore 0:
  11.4 113.3 all-reduce.17
  137.1 110.8 all-reduce.19
  261.9 110.6 all-reduce.21
  386.5 110.6 all-reduce.23
  511.2 110.6 all-reduce.25
  635.8 110.6 all-reduce.27
  760.4 110.6 all-reduce.29
  874.3 50.9 all-reduce.31
  1456.2 75.6 all-gather.1
  1540.1 106.8 all-reduce.33
  1661.1 109.7 all-reduce.35
  1786.8 109.7 all-reduce.37
  1912.5 109.7 all-reduce.39
  2038.3 109.7 all-reduce.41
  2164.0 109.6 all-reduce.43
  2276.7 23.4 reduce-scatter.7
  2303.2 33.2 reduce-scatter.5
  2339.7 31.9 reduce-scatter.3
where the time goes:
time: 2380 us
  waiting for transfers between devices  1670 us (70%)
  blocking collectives  518 us (22%)
  matrix products  70.9 us (3%)
  other arithmetic  53.3 us (2%)
  starting transfers between devices  28.3 us (1%)
    psum x13, waiting for transfers between devices, reduce_rows(): summed = lax.psum(partial_value, 'mp')  1420 us
    psum x2, blocking collectives, on_device(): lax.psum((jnp.sum(jnp.exp(logits - peak[..., None]), axis=-1), target_loc...  393 us
    pmax x1, blocking collectives, on_device(): peak = lax.pmax(local_peak, ('segment', 'mp'))  125 us
    all_gather x1, waiting for transfers between devices, on_device(): dnorm = lax.all_gather(norm_share, ('segment', 'mp'), axis=2, tiled=True)  75.1 us
    ppermute x12, waiting for transfers between devices, shifted(): return lax.ppermute(block, axis, route)  70.4 us
    psum x1, waiting for transfers between devices, broadcast(): return lax.psum(jnp.where(mine, x, jnp.zeros_like(x)), axis)  49.1 us
  transfers between devices with their start and end apart: 30, of which 29 were waited for; matrix products, arithmetic and copies ran while one was open for 2% of the time, Pallas kernels for 0%

commit v1 on v0

v1 whole, which is shorter than its diff:
```python
import jax
import jax.numpy as jnp
from jax import lax
from jax.experimental import pallas as pl
from jax.experimental.pallas import tpu as pltpu
from jax.sharding import PartitionSpec as P

MESH = pl.DeviceIdType.MESH
F32 = jnp.float32
BF16 = jnp.bfloat16

(
    G_FRS, G_FAG, G_FINY, G_FINZ, G_STAT, G_NRS, G_NY, G_NAG, G_BRS, G_BAG, G_TEXT, G_LOSS, G_SIBW,
) = range(13)
N_GROUPS = 13


def gelu_parts(pre_vals):
    coeff = 0.7978845608
    inner = coeff * (pre_vals + 0.044715 * pre_vals * pre_vals * pre_vals)
    tanh_val = jnp.tanh(inner)
    value = 0.5 * pre_vals * (1.0 + tanh_val)
    slope = 0.5 * (1.0 + tanh_val) + 0.5 * pre_vals * (1.0 - tanh_val * tanh_val) * coeff * (
        1.0 + 3.0 * 0.044715 * pre_vals * pre_vals
    )
    return (value, slope)


def row_scale(floats):
    return lax.rsqrt(jnp.mean(floats * floats, axis=-1, keepdims=True) + 1e-06)


def nn(a, b):
    return jnp.dot(a, b, preferred_element_type=F32)


def nt(a, b):
    return lax.dot_general(a, b, (((1,), (1,)), ((), ())), preferred_element_type=F32)


def tn(a, b):
    return lax.dot_general(a, b, (((0,), (0,)), ((), ())), preferred_element_type=F32)


def make_kernel(n_seg, n_z, n_dp, chunks, rows, width, hid_dev, voc_dev, units, denom):
    own_rows = rows // n_z
    n_peer = n_seg * n_z

    def kernel(
        text, dur, tgt, w_in, w_out, w_unit,
        loss_o, gin_o, gout_o, gun_o,
        wi_sib, wo_sib, wu_sib,
        xbuf, normed, part, rsf, osh, hid, slo,
        fin, fn, lg, cnt, stb, dlb, partd, rsd, ysend, yrecv, dxb, dsh,
        dpre, partb, rsb, bsh,
        gs_sib, gr_sib, gi_sib, gir_sib, gu_f, gu_sib, gur_sib, go_f, gi_f,
        xs_u, xr_u, xs_o, xr_o, xs_i, xr_i,
        lvec, lown, lrcv,
        ssem, rsem, sib_s, sib_r, dp_s, dp_r,
    ):
        s = lax.axis_index("segment")
        mp = lax.axis_index("mp")
        d = lax.axis_index("dp")
        z = lax.div(mp, 2)
        c = lax.rem(mp, 2)
        sib = 2 * z + (1 - c)
        me = s * n_z + z

        def rds(k, zz):
            return pl.ds(pl.multiple_of(k * rows + zz * own_rows, own_rows), own_rows)

        def kds(k):
            return pl.ds(pl.multiple_of(k * rows, rows), rows)

        def put(src, dst, a, b, where):
            pltpu.make_async_remote_copy(
                src_ref=src, dst_ref=dst, send_sem=a, recv_sem=b, device_id=where, device_id_type=MESH
            ).start()

        def drain(ref, sem):
            pltpu.make_async_copy(ref, ref, sem).wait()

        def peers_z(fn_of):
            def step(off, carry):
                fn_of(lax.rem(z + off, n_z))
                return carry

            lax.fori_loop(1, n_z, step, 0)

        def over(n, fn_of):
            def step(i, carry):
                fn_of(i)
                return carry

            lax.fori_loop(0, n, step, 0)

        barrier = pltpu.get_barrier_semaphore()

        def hello(off, carry):
            other = lax.rem(me + off, n_peer)
            pl.semaphore_signal(
                barrier, inc=1,
                device_id={"segment": lax.div(other, n_z), "mp": 2 * lax.rem(other, n_z) + c},
                device_id_type=MESH,
            )
            return carry

        lax.fori_loop(1, n_peer, hello, 0)

        def hello_dp(off, carry):
            pl.semaphore_signal(
                barrier, inc=1, device_id={"dp": lax.rem(d + off, n_dp)}, device_id_type=MESH
            )
            return carry

        lax.fori_loop(1, n_dp, hello_dp, 0)
        pl.semaphore_signal(barrier, inc=1, device_id={"mp": sib}, device_id_type=MESH)
        pl.semaphore_wait(barrier, n_peer - 1 + n_dp - 1 + 1)

        put(w_in, wi_sib, ssem.at[G_SIBW, 0], rsem.at[G_SIBW, 0], {"mp": sib})
        put(w_out, wo_sib, ssem.at[G_SIBW, 1], rsem.at[G_SIBW, 1], {"mp": sib})
        put(w_unit, wu_sib, ssem.at[G_LOSS, 1], rsem.at[G_LOSS, 1], {"mp": sib})

        @pl.when(s == 0)
        def _():
            def load(k):
                pltpu.make_async_copy(
                    text.at[chunks * c + k], xbuf.at[kds(k)], rsem.at[G_TEXT, k]
                ).start()

            over(chunks, load)

        def forward(k):
            @pl.when(s == 0)
            def _():
                drain(xbuf.at[kds(k)], rsem.at[G_TEXT, k])

            @pl.when(s > 0)
            def _():
                drain(xbuf.at[kds(k)], rsem.at[G_FAG, k])

            x = xbuf[kds(k), :].astype(F32)
            n = (x * row_scale(x)).astype(BF16)
            normed[kds(k), :] = n

            value, slope = gelu_parts(nn(n, w_in[...]))
            h0 = value.astype(BF16)
            hid[0, kds(k), :] = h0
            slo[0, kds(k), :] = slope
            acc = nn(h0, w_out[...])

            @pl.when(k == 0)
            def _():
                drain(wi_sib, rsem.at[G_SIBW, 0])
                drain(wo_sib, rsem.at[G_SIBW, 1])

            value, slope = gelu_parts(nn(n, wi_sib[...]))
            h1 = value.astype(BF16)
            hid[1, kds(k), :] = h1
            slo[1, kds(k), :] = slope
            acc = acc + nn(h1, wo_sib[...])
            part[kds(k), :] = acc.astype(BF16)
            rsf[k, z] = part[rds(k, z), :]
            peers_z(
                lambda z2: put(
                    part.at[rds(k, z2)], rsf.at[k, z], ssem.at[G_FRS, k], rsem.at[G_FRS, k],
                    {"mp": 2 * z2 + c},
                )
            )

        over(chunks, forward)

        def count(k):
            lengths = dur[chunks * c + k].astype(F32)
            lane = lax.broadcasted_iota(jnp.int32, (rows, rows), 1)
            sub = lax.broadcasted_iota(jnp.int32, (rows, rows), 0)
            tri = jnp.where(sub <= lane, 1.0, 0.0).astype(BF16)
            wide = jnp.broadcast_to(lengths, (8, rows)).astype(BF16)
            ends = nn(wide, tri)[0:1, :]
            starts = ends - lengths
            unit = lax.broadcasted_iota(jnp.int32, (units, rows), 0).astype(F32)
            onehot = jnp.where((starts <= unit) & (unit < ends), 1.0, 0.0).astype(BF16)
            target = tgt[chunks * c + k]
            ids = lax.broadcasted_iota(jnp.int32, (voc_dev, units), 0)
            for h, owner in ((0, mp), (1, sib)):
                first = (s * (2 * n_z) + owner) * voc_dev
                hits = jnp.where(ids + first == target, 1.0, 0.0).astype(BF16)
                cnt[k, h] = nn(hits, onehot)

        over(chunks, count)

        def owned_sum(buf, k):
            total = buf[k, 0].astype(F32)
            for i in range(1, n_z):
                total = total + buf[k, i].astype(F32)
            return total

        def forward_end(k):
            drain(rsf.at[k, pl.ds(0, n_z - 1)], rsem.at[G_FRS, k])
            x = xbuf[rds(k, z), :].astype(F32)
            new = (x + owned_sum(rsf, k)).astype(BF16)
            osh[k] = new

            @pl.when(s < n_seg - 1)
            def _():
                def send(z2):
                    put(
                        osh.at[k], xbuf.at[rds(k, z)], ssem.at[G_FAG, k], rsem.at[G_FAG, k],
                        {"segment": s + 1, "mp": 2 * z2 + c},
                    )

                over(n_z, lambda i: send(lax.rem(z + i, n_z)))

            @pl.when(s == n_seg - 1)
            def _():
                fin[rds(k, z), :] = new

                def send(y2):
                    put(
                        osh.at[k], fin.at[rds(k, z)], ssem.at[G_FINY, k], rsem.at[G_FINY, k],
                        {"segment": y2},
                    )

                over(n_seg - 1, send)

        over(chunks, forward_end)

        def relay(k):
            @pl.when(s < n_seg - 1)
            def _():
                drain(fin.at[rds(k, z)], rsem.at[G_FINY, k])

            peers_z(
                lambda z2: put(
                    fin.at[rds(k, z)], fin.at[rds(k, z)], ssem.at[G_FINZ, k], rsem.at[G_FINZ, k],
                    {"mp": 2 * z2 + c},
                )
            )

        over(chunks, relay)
        drain(wu_sib, rsem.at[G_LOSS, 1])

        def logits(k):
            drain(rsf.at[k, pl.ds(0, n_z - 1)], rsem.at[G_FINZ, k])
            x = fin[kds(k), :].astype(F32)
            n = (x * row_scale(x)).astype(BF16)
            fn[kds(k), :] = n
            a = nt(w_unit[...], n)
            b = nt(wu_sib[...], n)
            lg[k, 0] = a
            lg[k, 1] = b
            peak = jnp.maximum(jnp.max(a, axis=0, keepdims=True), jnp.max(b, axis=0, keepdims=True))
            total = jnp.sum(jnp.exp(a - peak), axis=0, keepdims=True) + jnp.sum(
                jnp.exp(b - peak), axis=0, keepdims=True
            )
            hit = jnp.sum(cnt[k, 0] * a, axis=0, keepdims=True) + jnp.sum(
                cnt[k, 1] * b, axis=0, keepdims=True
            )
            sub = lax.broadcasted_iota(jnp.int32, (8, rows), 0)
            stb[k, me] = jnp.where(sub == 0, peak, jnp.where(sub == 1, total, hit))

            def send(off, carry):
                other = lax.rem(me + off, n_peer)
                put(
                    stb.at[k, me], stb.at[k, me], ssem.at[G_STAT, k], rsem.at[G_STAT, k],
                    {"segment": lax.div(other, n_z), "mp": 2 * lax.rem(other, n_z) + c},
                )
                return carry

            lax.fori_loop(1, n_peer, send, 0)

        over(chunks, logits)

        lvec[...] = jnp.zeros_like(lvec)

        def dlogits(k):
            drain(stb.at[k, pl.ds(0, n_peer - 1)], rsem.at[G_STAT, k])
            every = stb[k]
            peaks = every[:, 0:1, :]
            peak = jnp.max(peaks, axis=0)
            total = jnp.sum(every[:, 1:2, :] * jnp.exp(peaks - peak[None]), axis=0)
            hit = jnp.sum(every[:, 2:3, :], axis=0)
            lse = peak + jnp.log(total)
            lengths = dur[chunks * c + k].astype(F32)
            lvec[0:1, :] += lengths * lse - hit
            acc = None
            for h, w in ((0, w_unit), (1, wu_sib)):
                grad = (lengths * jnp.exp(lg[k, h] - lse) - cnt[k, h]) * (1.0 / denom)
                grad = grad.astype(BF16)
                dlb[h, k] = grad
                term = tn(grad, w[...])
                acc = term if acc is None else acc + term
            partd[kds(k), :] = acc.astype(BF16)
            rsd[k, z] = partd[rds(k, z), :]
            peers_z(
                lambda z2: put(
                    partd.at[rds(k, z2)], rsd.at[k, z], ssem.at[G_NRS, k], rsem.at[G_NRS, k],
                    {"mp": 2 * z2 + c},
                )
            )

        over(chunks, dlogits)

        lown[...] = jnp.broadcast_to(jnp.sum(lvec[...], keepdims=True), lown.shape)
        put(lown, lrcv, ssem.at[G_LOSS, 0], rsem.at[G_LOSS, 0], {"mp": sib})

        quarter = width // n_dp
        for h in (1, 0):
            total = nn(dlb[h, 0], fn[pl.ds(0, rows), :])
            for k in range(1, chunks):
                total = total + nn(dlb[h, k], fn[pl.ds(k * rows, rows), :])
            for q in range(n_dp):
                piece = total[:, q * quarter : (q + 1) * quarter]
                if h == 1:
                    gu_sib[q] = piece.astype(BF16)
                else:
                    gu_f[q] = piece
            if h == 1:
                put(gu_sib, gur_sib, sib_s.at[0], sib_r.at[0], {"mp": sib})

        def norm_sum(k):
            drain(rsd.at[k, pl.ds(0, n_z - 1)], rsem.at[G_NRS, k])
            total = owned_sum(rsd, k)
            ysend[k] = total.astype(BF16)

            @pl.when(s < n_seg - 1)
            def _():
                put(
                    ysend.at[k], yrecv.at[k, s], ssem.at[G_NY, k], rsem.at[G_NY, k],
                    {"segment": n_seg - 1},
                )

        over(chunks, norm_sum)

        @pl.when(s == n_seg - 1)
        def _():
            def norm_end(k):
                drain(yrecv.at[k], rsem.at[G_NY, k])
                total = ysend[k].astype(F32)
                for i in range(n_seg - 1):
                    total = total + yrecv[k, i].astype(F32)
                g = total.astype(BF16).astype(F32)
                x = fin[rds(k, z), :].astype(F32)
                scale = row_scale(x)
                n = x * scale
                grad = scale * (g - n * jnp.mean(g * n, axis=-1, keepdims=True))
                grad = grad.astype(BF16)
                dsh[k] = grad
                dxb[rds(k, z), :] = grad
                peers_z(
                    lambda z2: put(
                        dsh.at[k], dxb.at[rds(k, z)], ssem.at[G_NAG, k], rsem.at[G_NAG, k],
                        {"mp": 2 * z2 + c},
                    )
                )

            over(chunks, norm_end)

        def dp_send(xs, xr, g):
            def step(off, carry):
                d2 = lax.rem(d + off, n_dp)
                put(xs.at[d2], xr.at[d], dp_s.at[g], dp_r.at[g], {"dp": d2})
                return carry

            lax.fori_loop(1, n_dp, step, 0)

        def dp_out(own, xr, g, out):
            drain(xr.at[pl.ds(0, n_dp - 1)], dp_r.at[g])
            total = own
            for off in range(1, n_dp):
                total = total + xr[lax.rem(d + off, n_dp)].astype(F32)
            out[...] = total

        drain(gur_sib, sib_r.at[0])

        def unit_sum(q):
            total = gu_f[q] + gur_sib[q].astype(F32)
            gu_f[q] = total
            xs_u[q] = total.astype(BF16)

        over(n_dp, unit_sum)
        dp_send(xs_u, xr_u, 0)

        def backward(k):
            @pl.when(s == n_seg - 1)
            def _():
                drain(rsf.at[k, pl.ds(0, n_z - 1)], rsem.at[G_NAG, k])

            @pl.when(s < n_seg - 1)
            def _():
                drain(dxb.at[kds(k)], rsem.at[G_BAG, k])

            g = dxb[kds(k), :]
            p0 = (nt(g, w_out[...]) * slo[0, kds(k), :]).astype(BF16)
            dpre[0, kds(k), :] = p0
            p1 = (nt(g, wo_sib[...]) * slo[1, kds(k), :]).astype(BF16)
            dpre[1, kds(k), :] = p1

            @pl.when(s > 0)
            def _():
                partb[kds(k), :] = (nt(p0, w_in[...]) + nt(p1, wi_sib[...])).astype(BF16)
                rsb[k, z] = partb[rds(k, z), :]
                peers_z(
                    lambda z2: put(
                        partb.at[rds(k, z2)], rsb.at[k, z], ssem.at[G_BRS, k], rsem.at[G_BRS, k],
                        {"mp": 2 * z2 + c},
                    )
                )

        over(chunks, backward)

        @pl.when(s > 0)
        def _():
            def backward_end(k):
                drain(rsb.at[k, pl.ds(0, n_z - 1)], rsem.at[G_BRS, k])
                g = owned_sum(rsb, k)
                x = xbuf[rds(k, z), :].astype(F32)
                scale = row_scale(x)
                n = x * scale
                back = scale * (g - n * jnp.mean(g * n, axis=-1, keepdims=True))
                bsh[k] = (dxb[rds(k, z), :].astype(F32) + back).astype(BF16)

                def send(z2):
                    put(
                        bsh.at[k], dxb.at[rds(k, z)], ssem.at[G_BAG, k], rsem.at[G_BAG, k],
                        {"segment": s - 1, "mp": 2 * z2 + c},
                    )

                over(n_z, lambda i: send(lax.rem(z + i, n_z)))

            over(chunks, backward_end)

        out_q = width // n_dp
        for q in range(n_dp):
            gs_sib[q] = tn(hid[1], dxb[:, q * out_q : (q + 1) * out_q]).astype(BF16)
        put(gs_sib, gr_sib, sib_s.at[1], sib_r.at[1], {"mp": sib})
        for q in range(n_dp):
            go_f[q] = tn(hid[0], dxb[:, q * out_q : (q + 1) * out_q])
        for q in range(n_dp):
            gi_sib[q] = tn(normed[:, q * out_q : (q + 1) * out_q], dpre[1]).astype(BF16)
        put(gi_sib, gir_sib, sib_s.at[2], sib_r.at[2], {"mp": sib})
        drain(gr_sib, sib_r.at[1])

        def out_sum(q):
            total = go_f[q] + gr_sib[q].astype(F32)
            go_f[q] = total
            xs_o[q] = total.astype(BF16)

        over(n_dp, out_sum)
        dp_send(xs_o, xr_o, 1)
        for q in range(n_dp):
            gi_f[q] = tn(normed[:, q * out_q : (q + 1) * out_q], dpre[0])
        drain(gir_sib, sib_r.at[2])

        def in_sum(q):
            total = gi_f[q] + gir_sib[q].astype(F32)
            gi_f[q] = total
            xs_i[q] = total.astype(BF16)

        over(n_dp, in_sum)
        dp_send(xs_i, xr_i, 2)

        dp_out(gu_f[d], xr_u, 0, gun_o)
        drain(lrcv, rsem.at[G_LOSS, 0])
        loss_o[...] = (lown[...] + lrcv[...]) * (1.0 / denom)
        dp_out(go_f[d], xr_o, 1, gout_o)
        dp_out(gi_f[d], xr_i, 2, gin_o)

        drain(w_in, ssem.at[G_SIBW, 0])
        drain(w_out, ssem.at[G_SIBW, 1])
        drain(w_unit, ssem.at[G_LOSS, 1])
        drain(lown, ssem.at[G_LOSS, 0])
        drain(gu_sib, sib_s.at[0])
        drain(gs_sib, sib_s.at[1])
        drain(gi_sib, sib_s.at[2])
        drain(xs_u.at[pl.ds(0, n_dp - 1)], dp_s.at[0])
        drain(xs_o.at[pl.ds(0, n_dp - 1)], dp_s.at[1])
        drain(xs_i.at[pl.ds(0, n_dp - 1)], dp_s.at[2])

        def finish(k):
            part_of = rsf.at[k, pl.ds(0, n_z - 1)]
            drain(part_of, ssem.at[G_FRS, k])
            drain(part_of, ssem.at[G_FINZ, k])
            drain(part_of, ssem.at[G_NRS, k])
            drain(stb.at[k, pl.ds(0, n_peer - 1)], ssem.at[G_STAT, k])

            @pl.when(s < n_seg - 1)
            def _():
                drain(rsf.at[k], ssem.at[G_FAG, k])
                drain(ysend.at[k], ssem.at[G_NY, k])

            @pl.when(s == n_seg - 1)
            def _():
                drain(yrecv.at[k], ssem.at[G_FINY, k])
                drain(part_of, ssem.at[G_NAG, k])

            @pl.when(s > 0)
            def _():
                drain(part_of, ssem.at[G_BRS, k])
                drain(rsf.at[k], ssem.at[G_BAG, k])

        over(chunks, finish)

    vm = pltpu.VMEM
    all_rows = chunks * rows
    shard = (chunks, own_rows, width)
    scatter = (chunks, n_z, own_rows, width)
    quarter = width // n_dp
    scratch = [
        vm((width, hid_dev), BF16), vm((hid_dev, width), BF16), vm((voc_dev, width), BF16),
        vm((all_rows, width), BF16), vm((all_rows, width), BF16), vm((all_rows, width), BF16),
        vm(scatter, BF16), vm(shard, BF16), vm((2, all_rows, hid_dev), BF16), vm((2, all_rows, hid_dev), F32),
        vm((all_rows, width), BF16), vm((all_rows, width), BF16),
        vm((chunks, 2, voc_dev, rows), F32), vm((chunks, 2, voc_dev, rows), F32),
        vm((chunks, n_peer, 8, rows), F32), vm((2, chunks, voc_dev, rows), BF16),
        vm((all_rows, width), BF16), vm(scatter, BF16), vm(shard, BF16),
        vm((chunks, n_seg - 1, own_rows, width), BF16), vm((all_rows, width), BF16), vm(shard, BF16),
        vm((2, all_rows, hid_dev), BF16), vm((all_rows, width), BF16), vm(scatter, BF16), vm(shard, BF16),
        vm((n_dp, hid_dev, quarter), BF16), vm((n_dp, hid_dev, quarter), BF16),
        vm((n_dp, quarter, hid_dev), BF16), vm((n_dp, quarter, hid_dev), BF16),
        vm((n_dp, voc_dev, quarter), F32), vm((n_dp, voc_dev, quarter), BF16), vm((n_dp, voc_dev, quarter), BF16),
        vm((n_dp, hid_dev, quarter), F32), vm((n_dp, quarter, hid_dev), F32),
        vm((n_dp, voc_dev, quarter), BF16), vm((n_dp, voc_dev, quarter), BF16),
        vm((n_dp, hid_dev, quarter), BF16), vm((n_dp, hid_dev, quarter), BF16),
        vm((n_dp, quarter, hid_dev), BF16), vm((n_dp, quarter, hid_dev), BF16),
        vm((8, rows), F32), vm((8, 128), F32), vm((8, 128), F32),
        pltpu.SemaphoreType.DMA((N_GROUPS, 2)), pltpu.SemaphoreType.DMA((N_GROUPS, 2)),
        pltpu.SemaphoreType.DMA((3,)), pltpu.SemaphoreType.DMA((3,)),
        pltpu.SemaphoreType.DMA((3,)), pltpu.SemaphoreType.DMA((3,)),
    ]
    return kernel, scratch


def solution(mesh):
    n_seg, n_mp, n_dp = mesh.shape["segment"], mesh.shape["mp"], mesh.shape["dp"]

    def on_device(text_rows, durations, unit_targets, w_in, w_out, w_unit):
        micro, rows, width = text_rows.shape
        units = unit_targets.shape[1]
        hid_dev = w_in.shape[2]
        voc_dev = w_unit.shape[1]
        denom = float(micro * units * n_dp)
        kernel, scratch = make_kernel(
            n_seg, n_mp // 2, n_dp, micro // 2, rows, width, hid_dev, voc_dev, units, denom
        )
        quarter = width // n_dp
        vmem = pl.BlockSpec(memory_space=pltpu.VMEM)
        loss, gin, gout, gun = pl.pallas_call(
            kernel,
            out_shape=(
                jax.ShapeDtypeStruct((8, 128), F32),
                jax.ShapeDtypeStruct((quarter, hid_dev), F32),
                jax.ShapeDtypeStruct((hid_dev, quarter), F32),
                jax.ShapeDtypeStruct((voc_dev, quarter), F32),
            ),
            in_specs=[pl.BlockSpec(memory_space=pl.ANY)] + [vmem] * 5,
            out_specs=(vmem,) * 4,
            scratch_shapes=scratch,
            compiler_params=pltpu.CompilerParams(
                collective_id=0, has_side_effects=True, vmem_limit_bytes=60 * 1024 * 1024
            ),
        )(
            text_rows, durations, unit_targets.reshape(micro, 1, units), w_in[0], w_out[0],
            jnp.transpose(w_unit),
        )
        return (loss[0, 0][None], gin[None], gout[None], jnp.transpose(gun))

    placed = (
        P(None, "dp", None),
        P(None, "dp", None),
        P(None, "dp"),
        P("segment", None, "mp"),
        P("segment", "mp", None),
        P(None, ("segment", "mp")),
    )
    return jax.shard_map(
        on_device,
        mesh=mesh,
        in_specs=placed,
        out_specs=(
            P("dp"),
            P("segment", "dp", "mp"),
            P("segment", "mp", "dp"),
            P("dp", ("segment", "mp")),
        ),
        check_vma=False,
    )
```

time: 2380 us -> 250 us (0.11)
  waiting for transfers between devices: 1670 us -> 0 us
  blocking collectives: 518 us -> 0 us
  Pallas kernels: 0 us -> 243 us
  matrix products: 70.9 us -> 0 us
  other arithmetic: 53.3 us -> 0 us
  starting transfers between devices: 28.3 us -> 0 us
    psum x14 -> x0, waiting for transfers between devices: 1470 us -> none  [the longest x13 1420 us: reduce_rows(): summed = lax.psum(partial_value, 'mp')]
    psum x2 -> x0, blocking collectives: 393 us -> none  [on_device(): lax.psum((jnp.sum(jnp.exp(logits - peak[..., None]), axis=-1), target_loc...]
    pallas_call x0 -> x1, Pallas kernels: none -> 243 us  [on_device(): pl.pallas_call(kernel, out_shape=(jax.ShapeDtypeStruct((8, 128), F32), ja...]
    pmax x1 -> x0, blocking collectives: 125 us -> none  [on_device(): peak = lax.pmax(local_peak, ('segment', 'mp'))]
    all_gather x1 -> x0, waiting for transfers between devices: 75.1 us -> none  [on_device(): dnorm = lax.all_gather(norm_share, ('segment', 'mp'), axis=2, tiled=True)]
    dot_general x44 -> x0, matrix products: 70.9 us -> none  [the longest x7 19.6 us: on_device(): jnp.dot(normed.T, dpre, preferred_element_type=jnp.float32)]
    ppermute x12 -> x0, waiting for transfers between devices: 70.4 us -> none  [shifted(): return lax.ppermute(block, axis, route)]
    reduce_scatter x3 -> x0, waiting for transfers between devices: 57.1 us -> none  [the longest x1 35.2 us: on_device(): lax.psum_scatter(grad_first, 'dp', scatter_dimension=0, tiled=True)]
  transfers between devices with their start and end apart: 30 -> 0, of which waited for: 29 -> 0; matrix products, arithmetic and copies ran while one was open for 2% -> 0% of each run, Pallas kernels for 0% -> 0%
where the time goes in v1:
time: 250 us
  Pallas kernels  243 us (97%)
  local copies, waits for them, and re-layouts  6.14 us (2%)
    pallas_call x1, Pallas kernels, on_device(): pl.pallas_call(kernel, out_shape=(jax.ShapeDtypeStruct((8, 128), F32), ja...  243 us

profile of v1, /device:TPU:1, one launch (start us, length us, event | category | flops | bytes accessed | tf_op | source)
XLA Modules:
  0.0 249.8 jit_solution(3011087077344603788)
XLA Ops:
  0.6 1.3 reshape.11.tgt
  1.9 243.0 %shard_map.93 = (f32[8,128]{1,0:T(8,128)}, f32[256,512]{1,0:T(8,128)}, f32[512,256]{1,0:T(8,128)}, f32[160,256]{1,0:T(8,128)}) custom-call(bf16[4,128,1024]{2,1,0:T(8,128)(2,1)} %text.1, s32[4,1,128]{2,1,0:T(1,128)} %dur.1, s32[4,1,512]{2,1,0:T(1,128)} %reshape.11.tgt, bf16[1024,512]{1,0:T(8,128)(2,1)} %bitcast.7, bf16[512,1024]{1,0:T(8,128)(2,1)} %bitcast.8, ...), custom_call_target="tpu_custom_call" | custom-call | tf_op jit(solution)/shard_map/pallas_call | solution.py:548
  245.0 1.2 slice.3
  246.1 0.0 copy-start
  246.1 1.9 copy.13
  248.1 0.0 copy-done
  248.1 0.0 copy-start.1
  248.1 0.8 copy.14
  248.9 0.3 copy-done.1
  249.1 0.7 copy.15
Async XLA Ops:
  246.1 1.9 copy-start
  248.1 1.1 copy-start.1

commit v2 on v1

v2 whole, which is shorter than its diff:
```python
import jax
import jax.numpy as jnp
from jax import lax
from jax.experimental import pallas as pl
from jax.experimental.pallas import tpu as pltpu
from jax.sharding import PartitionSpec as P

MESH = pl.DeviceIdType.MESH
F32 = jnp.float32
BF16 = jnp.bfloat16

(
    G_FRS, G_FAG, G_FINY, G_FINZ, G_STAT, G_NRS, G_NY, G_NAG, G_BRS, G_BAG, G_TEXT, G_LOSS, G_SIBW,
) = range(13)
N_GROUPS = 13


def gelu_parts(pre_vals):
    coeff = 0.7978845608
    inner = coeff * (pre_vals + 0.044715 * pre_vals * pre_vals * pre_vals)
    tanh_val = jnp.tanh(inner)
    value = 0.5 * pre_vals * (1.0 + tanh_val)
    slope = 0.5 * (1.0 + tanh_val) + 0.5 * pre_vals * (1.0 - tanh_val * tanh_val) * coeff * (
        1.0 + 3.0 * 0.044715 * pre_vals * pre_vals
    )
    return (value, slope)


def row_scale(floats):
    return lax.rsqrt(jnp.mean(floats * floats, axis=-1, keepdims=True) + 1e-06)


def norm_back(floats, grads):
    scale = row_scale(floats)
    normal = floats * scale
    return scale * (grads - normal * jnp.mean(grads * normal, axis=-1, keepdims=True))


def nn(a, b):
    return jnp.dot(a, b, preferred_element_type=F32)


def nt(a, b):
    return lax.dot_general(a, b, (((1,), (1,)), ((), ())), preferred_element_type=F32)


def tn(a, b):
    return lax.dot_general(a, b, (((0,), (0,)), ((), ())), preferred_element_type=F32)


def make_kernel(n_seg, n_z, n_dp, micros, chunks, rows, width, hid_dev, voc_dev, units, denom):
    all_rows = micros * rows
    cut = all_rows // chunks
    per = chunks // micros
    col = width // n_z
    n_peer = n_seg * n_z
    quarter = width // n_dp
    blocks = n_z // n_dp

    def kernel(
        text, dur, tgt, w_in, w_out, w_unit,
        loss_o, gin_o, gout_o, gun_o,
        wi_sib, wo_sib, wu_sib,
        xbuf, normed, part, rsf, osh, hid, slo,
        fin, fn, lg, cnt, stb, dlb, partd, rsd, ysend, yrecv, dxb, dsh,
        dpre, partb, rsb, bsh,
        gs_sib, gr_sib, gi_sib, gir_sib, gu_f, gu_sib, gur_sib, go_f, gi_f,
        xs_u, xr_u, xs_o, xr_o, xs_i, xr_i,
        lvec, lown, lrcv,
        ssem, rsem, sib_s, sib_r, dp_s, dp_r,
    ):
        s = lax.axis_index("segment")
        mp = lax.axis_index("mp")
        d = lax.axis_index("dp")
        z = lax.div(mp, 2)
        c = lax.rem(mp, 2)
        sib = 2 * z + (1 - c)
        me = s * n_z + z
        last = n_seg - 1

        def cds(k):
            return pl.ds(pl.multiple_of(k * cut, cut), cut)

        def mds(m):
            return pl.ds(pl.multiple_of(m * rows, rows), rows)

        def whole(buf, where):
            return jnp.concatenate([buf[i, where, :] for i in range(n_z)], axis=-1)

        def columns(i):
            return slice(i * col, (i + 1) * col)

        def put(src, dst, a, b, where):
            pltpu.make_async_remote_copy(
                src_ref=src, dst_ref=dst, send_sem=a, recv_sem=b, device_id=where, device_id_type=MESH
            ).start()

        def drain(ref, sem):
            pltpu.make_async_copy(ref, ref, sem).wait()

        def over(n, fn_of):
            def step(i, carry):
                fn_of(i)
                return carry

            lax.fori_loop(0, n, step, 0)

        def peers_z(fn_of):
            def step(i):
                side = 1 - 2 * lax.rem(i, 2)
                off = n_z // 2 + side * lax.div(i + 1, 2)
                fn_of(lax.rem(z + off, n_z))

            over(n_z - 1, step)

        barrier = pltpu.get_barrier_semaphore()

        def greet(where):
            pl.semaphore_signal(barrier, inc=1, device_id=where, device_id_type=MESH)

        peers_z(lambda z2: greet({"mp": 2 * z2 + c}))
        over(n_seg - 1, lambda i: greet({"segment": lax.rem(s + i + 1, n_seg)}))
        over(n_dp - 1, lambda i: greet({"dp": lax.rem(d + i + 1, n_dp)}))
        greet({"mp": sib})

        @pl.when(s == 0)
        def _():
            def load(k):
                for i in range(n_z):
                    pltpu.make_async_copy(
                        text.at[
                            micros * c + lax.div(k, per),
                            pl.ds(pl.multiple_of(lax.rem(k, per) * cut, cut), cut),
                            pl.ds(i * col, col),
                        ],
                        xbuf.at[i, cds(k)],
                        rsem.at[G_TEXT, k],
                    ).start()

            over(chunks, load)

        def count(k):
            lengths = dur[micros * c + k].astype(F32)
            lane = lax.broadcasted_iota(jnp.int32, (rows, rows), 1)
            sub = lax.broadcasted_iota(jnp.int32, (rows, rows), 0)
            tri = jnp.where(sub <= lane, 1.0, 0.0).astype(BF16)
            wide = jnp.broadcast_to(lengths, (8, rows)).astype(BF16)
            ends = nn(wide, tri)[0:1, :]
            starts = ends - lengths
            unit = lax.broadcasted_iota(jnp.int32, (units, rows), 0).astype(F32)
            onehot = jnp.where((starts <= unit) & (unit < ends), 1.0, 0.0).astype(BF16)
            target = tgt[pl.ds(micros * c + k, 1), :]
            ids = lax.broadcasted_iota(jnp.int32, (voc_dev, units), 0)
            for h, owner in ((0, mp), (1, sib)):
                first = (s * (2 * n_z) + owner) * voc_dev
                hits = jnp.where(ids + first == target, 1.0, 0.0).astype(BF16)
                cnt[k, h] = nn(hits, onehot)

        over(micros, count)
        pl.semaphore_wait(barrier, n_z - 1 + n_seg - 1 + n_dp - 1 + 1)

        put(w_in, wi_sib, ssem.at[G_SIBW, 0], rsem.at[G_SIBW, 0], {"mp": sib})
        put(w_out, wo_sib, ssem.at[G_SIBW, 1], rsem.at[G_SIBW, 1], {"mp": sib})
        put(w_unit, wu_sib, ssem.at[G_LOSS, 1], rsem.at[G_LOSS, 1], {"mp": sib})

        def scatter_z(buf, got, where, slot, group, k):
            own = got.at[slot, z]
            got[slot, z] = buf[z, where, :]
            peers_z(
                lambda z2: put(
                    buf.at[z2, where], own, ssem.at[group, k], rsem.at[group, k], {"mp": 2 * z2 + c}
                )
            )

        def owned_sum(buf, k):
            total = buf[k, 0].astype(F32)
            for i in range(1, n_z):
                total = total + buf[k, i].astype(F32)
            return total

        def forward(k):
            @pl.when(s == 0)
            def _():
                drain(xbuf.at[:, cds(k)], rsem.at[G_TEXT, k])

            @pl.when(s > 0)
            def _():
                drain(xbuf.at[:, cds(k)], rsem.at[G_FAG, k])

            x = whole(xbuf, cds(k)).astype(F32)
            n = (x * row_scale(x)).astype(BF16)
            normed[cds(k), :] = n

            value, slope = gelu_parts(nn(n, w_in[...]))
            h0 = value.astype(BF16)
            hid[0, cds(k), :] = h0
            slo[0, cds(k), :] = slope
            acc = nn(h0, w_out[...])

            @pl.when(k == 0)
            def _():
                drain(wi_sib, rsem.at[G_SIBW, 0])
                drain(wo_sib, rsem.at[G_SIBW, 1])

            value, slope = gelu_parts(nn(n, wi_sib[...]))
            h1 = value.astype(BF16)
            hid[1, cds(k), :] = h1
            slo[1, cds(k), :] = slope
            acc = (acc + nn(h1, wo_sib[...])).astype(BF16)
            for i in range(n_z):
                part[i, cds(k), :] = acc[:, columns(i)]
            scatter_z(part, rsf, cds(k), k, G_FRS, k)

        def forward_end(k):
            drain(rsf.at[k, pl.ds(0, n_z - 1)], rsem.at[G_FRS, k])
            x = xbuf[z, cds(k), :].astype(F32)
            new = (x + owned_sum(rsf, k)).astype(BF16)
            osh[k] = new

            @pl.when(s < last)
            def _():
                def send(z2):
                    put(
                        osh.at[k], xbuf.at[z, cds(k)], ssem.at[G_FAG, k], rsem.at[G_FAG, k],
                        {"segment": s + 1, "mp": 2 * z2 + c},
                    )

                peers_z(send)
                send(z)

            @pl.when(s == last)
            def _():
                fin[z, cds(k), :] = new

                def send(y2):
                    put(
                        osh.at[k], fin.at[z, cds(k)], ssem.at[G_FINY, k], rsem.at[G_FINY, k],
                        {"segment": y2},
                    )

                over(n_seg - 1, send)

        def staged(first, second):
            def step(i):
                @pl.when(i < chunks)
                def _():
                    first(i)

                @pl.when(i > 0)
                def _():
                    second(i - 1)

            over(chunks + 1, step)

        staged(forward, forward_end)
        drain(wu_sib, rsem.at[G_LOSS, 1])
        lvec[...] = jnp.zeros_like(lvec)

        def relay(k):
            @pl.when(s < last)
            def _():
                drain(fin.at[z, cds(k)], rsem.at[G_FINY, k])

            peers_z(
                lambda z2: put(
                    fin.at[z, cds(k)], fin.at[z, cds(k)], ssem.at[G_FINZ, k], rsem.at[G_FINZ, k],
                    {"mp": 2 * z2 + c},
                )
            )

        def logits(k):
            for j in range(per):
                drain(rsf.at[0, pl.ds(0, n_z - 1)], rsem.at[G_FINZ, k * per + j])
            x = whole(fin, mds(k)).astype(F32)
            n = (x * row_scale(x)).astype(BF16)
            fn[mds(k), :] = n
            a = nt(w_unit[...], n)
            b = nt(wu_sib[...], n)
            lg[k, 0] = a
            lg[k, 1] = b
            peak = jnp.maximum(jnp.max(a, axis=0, keepdims=True), jnp.max(b, axis=0, keepdims=True))
            total = jnp.sum(jnp.exp(a - peak), axis=0, keepdims=True) + jnp.sum(
                jnp.exp(b - peak), axis=0, keepdims=True
            )
            hit = jnp.sum(cnt[k, 0] * a, axis=0, keepdims=True) + jnp.sum(
                cnt[k, 1] * b, axis=0, keepdims=True
            )
            sub = lax.broadcasted_iota(jnp.int32, (8, rows), 0)
            stb[k, me] = jnp.where(sub == 0, peak, jnp.where(sub == 1, total, hit))

            def send(off):
                other = lax.rem(me + off + 1, n_peer)
                put(
                    stb.at[k, me], stb.at[k, me], ssem.at[G_STAT, k], rsem.at[G_STAT, k],
                    {"segment": lax.div(other, n_z), "mp": 2 * lax.rem(other, n_z) + c},
                )

            over(n_peer - 1, send)

        def dlogits(k):
            drain(stb.at[k, pl.ds(0, n_peer - 1)], rsem.at[G_STAT, k])
            every = stb[k]
            peaks = every[:, 0:1, :]
            peak = jnp.max(peaks, axis=0)
            total = jnp.sum(every[:, 1:2, :] * jnp.exp(peaks - peak[None]), axis=0)
            hit = jnp.sum(every[:, 2:3, :], axis=0)
            lse = peak + jnp.log(total)
            lengths = dur[micros * c + k].astype(F32)
            lvec[0:1, :] += lengths * lse - hit
            acc = None
            for h, w in ((0, w_unit), (1, wu_sib)):
                grad = (lengths * jnp.exp(lg[k, h] - lse) - cnt[k, h]) * (1.0 / denom)
                grad = grad.astype(BF16)
                dlb[h, k] = grad
                term = tn(grad, w[...])
                acc = term if acc is None else acc + term
            x = whole(fin, mds(k)).astype(F32)
            acc = norm_back(x, acc).astype(BF16)
            for i in range(n_z):
                partd[i, mds(k), :] = acc[:, columns(i)]
            scatter_z(partd, rsd, mds(k), k, G_NRS, k)

        def norm_sum(k):
            drain(rsd.at[k, pl.ds(0, n_z - 1)], rsem.at[G_NRS, k])
            ysend[k] = owned_sum(rsd, k).astype(BF16)

            @pl.when(s < last)
            def _():
                put(ysend.at[k], yrecv.at[k, s], ssem.at[G_NY, k], rsem.at[G_NY, k], {"segment": last})

        def norm_end(k):
            @pl.when(s == last)
            def _():
                drain(yrecv.at[k], rsem.at[G_NY, k])
                total = ysend[k].astype(F32)
                for i in range(n_seg - 1):
                    total = total + yrecv[k, i].astype(F32)
                grad = total.astype(BF16)
                dsh[k] = grad
                dxb[z, mds(k), :] = grad
                peers_z(
                    lambda z2: put(
                        dsh.at[k], dxb.at[z, mds(k)], ssem.at[G_NAG, k], rsem.at[G_NAG, k],
                        {"mp": 2 * z2 + c},
                    )
                )

        def dp_send(xs, xr, g):
            def step(off):
                d2 = lax.rem(d + off + 1, n_dp)
                put(xs.at[d2], xr.at[d], dp_s.at[g], dp_r.at[g], {"dp": d2})

            over(n_dp - 1, step)

        def dp_out(own, xr, g, out):
            drain(xr.at[pl.ds(0, n_dp - 1)], dp_r.at[g])
            total = own
            for off in range(1, n_dp):
                total = total + xr[lax.rem(d + off, n_dp)].astype(F32)
            out[...] = total

        def unit_grad():
            lown[...] = jnp.broadcast_to(jnp.sum(lvec[...], keepdims=True), lown.shape)
            put(lown, lrcv, ssem.at[G_LOSS, 0], rsem.at[G_LOSS, 0], {"mp": sib})
            for h in (1, 0):
                total = nn(dlb[h, 0], fn[pl.ds(0, rows), :])
                for k in range(1, micros):
                    total = total + nn(dlb[h, k], fn[pl.ds(k * rows, rows), :])
                for q in range(n_dp):
                    piece = total[:, q * quarter : (q + 1) * quarter]
                    if h == 1:
                        gu_sib[q] = piece.astype(BF16)
                    else:
                        gu_f[q] = piece
                if h == 1:
                    put(gu_sib, gur_sib, sib_s.at[0], sib_r.at[0], {"mp": sib})
            drain(gur_sib, sib_r.at[0])

            def unit_sum(q):
                total = gu_f[q] + gur_sib[q].astype(F32)
                gu_f[q] = total
                xs_u[q] = total.astype(BF16)

            over(n_dp, unit_sum)
            dp_send(xs_u, xr_u, 0)

        for k in range(per + 1):
            relay(k)
        logits(0)
        for k in range(per + 1, chunks):
            relay(k)
        dlogits(0)
        logits(1)
        norm_sum(0)
        dlogits(1)
        norm_end(0)
        norm_sum(1)
        norm_end(1)

        @pl.when(s < last)
        def _():
            unit_grad()

        def backward(k):
            @pl.when((s == last) & (lax.rem(k, per) == 0))
            def _():
                drain(rsd.at[0, pl.ds(0, n_z - 1)], rsem.at[G_NAG, lax.div(k, per)])

            @pl.when(s < last)
            def _():
                drain(dxb.at[:, cds(k)], rsem.at[G_BAG, k])

            g = whole(dxb, cds(k))
            p0 = (nt(g, w_out[...]) * slo[0, cds(k), :]).astype(BF16)
            dpre[0, cds(k), :] = p0
            p1 = (nt(g, wo_sib[...]) * slo[1, cds(k), :]).astype(BF16)
            dpre[1, cds(k), :] = p1

            @pl.when(s > 0)
            def _():
                x = whole(xbuf, cds(k)).astype(F32)
                acc = norm_back(x, nt(p0, w_in[...]) + nt(p1, wi_sib[...])).astype(BF16)
                for i in range(n_z):
                    partb[i, cds(k), :] = acc[:, columns(i)]
                scatter_z(partb, rsb, cds(k), k, G_BRS, k)

        def backward_end(k):
            @pl.when(s > 0)
            def _():
                drain(rsb.at[k, pl.ds(0, n_z - 1)], rsem.at[G_BRS, k])
                bsh[k] = (dxb[z, cds(k), :].astype(F32) + owned_sum(rsb, k)).astype(BF16)

                def send(z2):
                    put(
                        bsh.at[k], dxb.at[z, cds(k)], ssem.at[G_BAG, k], rsem.at[G_BAG, k],
                        {"segment": s - 1, "mp": 2 * z2 + c},
                    )

                peers_z(send)
                send(z)

        staged(backward, backward_end)

        @pl.when(s == last)
        def _():
            unit_grad()

        def grad_columns(q):
            return jnp.concatenate([dxb[q * blocks + i] for i in range(blocks)], axis=-1)

        for q in range(n_dp):
            gs_sib[q] = tn(hid[1], grad_columns(q)).astype(BF16)
        put(gs_sib, gr_sib, sib_s.at[1], sib_r.at[1], {"mp": sib})
        for q in range(n_dp):
            go_f[q] = tn(hid[0], grad_columns(q))
        for q in range(n_dp):
            gi_sib[q] = tn(normed[:, q * quarter : (q + 1) * quarter], dpre[1]).astype(BF16)
        put(gi_sib, gir_sib, sib_s.at[2], sib_r.at[2], {"mp": sib})
        drain(gr_sib, sib_r.at[1])

        def out_sum(q):
            total = go_f[q] + gr_sib[q].astype(F32)
            go_f[q] = total
            xs_o[q] = total.astype(BF16)

        over(n_dp, out_sum)
        dp_send(xs_o, xr_o, 1)
        for q in range(n_dp):
            gi_f[q] = tn(normed[:, q * quarter : (q + 1) * quarter], dpre[0])
        drain(gir_sib, sib_r.at[2])

        def in_sum(q):
            total = gi_f[q] + gir_sib[q].astype(F32)
            gi_f[q] = total
            xs_i[q] = total.astype(BF16)

        over(n_dp, in_sum)
        dp_send(xs_i, xr_i, 2)

        dp_out(gu_f[d], xr_u, 0, gun_o)
        drain(lrcv, rsem.at[G_LOSS, 0])
        loss_o[0] = jnp.max(lown[...] + lrcv[...]) * (1.0 / denom)
        dp_out(go_f[d], xr_o, 1, gout_o)
        dp_out(gi_f[d], xr_i, 2, gin_o)

        drain(w_in, ssem.at[G_SIBW, 0])
        drain(w_out, ssem.at[G_SIBW, 1])
        drain(w_unit, ssem.at[G_LOSS, 1])
        drain(lown, ssem.at[G_LOSS, 0])
        drain(gu_sib, sib_s.at[0])
        drain(gs_sib, sib_s.at[1])
        drain(gi_sib, sib_s.at[2])
        drain(xs_u.at[pl.ds(0, n_dp - 1)], dp_s.at[0])
        drain(xs_o.at[pl.ds(0, n_dp - 1)], dp_s.at[1])
        drain(xs_i.at[pl.ds(0, n_dp - 1)], dp_s.at[2])

        def finish(k):
            part_of = rsf.at[0, pl.ds(0, n_z - 1)]
            drain(part_of, ssem.at[G_FRS, k])
            drain(part_of, ssem.at[G_FINZ, k])

            @pl.when(s < last)
            def _():
                drain(rsf.at[0], ssem.at[G_FAG, k])

            @pl.when(s == last)
            def _():
                drain(osh.at[pl.ds(0, n_seg - 1)], ssem.at[G_FINY, k])

            @pl.when(s > 0)
            def _():
                drain(part_of, ssem.at[G_BRS, k])
                drain(rsf.at[0], ssem.at[G_BAG, k])

        def finish_micro(k):
            part_of = rsd.at[0, pl.ds(0, n_z - 1)]
            drain(part_of, ssem.at[G_NRS, k])
            drain(stb.at[k, pl.ds(0, n_peer - 1)], ssem.at[G_STAT, k])

            @pl.when(s < last)
            def _():
                drain(ysend.at[k], ssem.at[G_NY, k])

            @pl.when(s == last)
            def _():
                drain(part_of, ssem.at[G_NAG, k])

        over(chunks, finish)
        over(micros, finish_micro)

    vm = pltpu.VMEM
    lines = (n_z, all_rows, col)
    shard = (chunks, cut, col)
    mshard = (micros, rows, col)
    scatter = (chunks, n_z, cut, col)
    mscatter = (micros, n_z, rows, col)
    scratch = [
        vm((width, hid_dev), BF16), vm((hid_dev, width), BF16), vm((voc_dev, width), BF16),
        vm(lines, BF16), vm((all_rows, width), BF16), vm(lines, BF16),
        vm(scatter, BF16), vm(shard, BF16), vm((2, all_rows, hid_dev), BF16), vm((2, all_rows, hid_dev), F32),
        vm(lines, BF16), vm((all_rows, width), BF16),
        vm((micros, 2, voc_dev, rows), F32), vm((micros, 2, voc_dev, rows), F32),
        vm((micros, n_peer, 8, rows), F32), vm((2, micros, voc_dev, rows), BF16),
        vm(lines, BF16), vm(mscatter, BF16), vm(mshard, BF16),
        vm((micros, n_seg - 1, rows, col), BF16), vm(lines, BF16), vm(mshard, BF16),
        vm((2, all_rows, hid_dev), BF16), vm(lines, BF16), vm(scatter, BF16), vm(shard, BF16),
        vm((n_dp, hid_dev, quarter), BF16), vm((n_dp, hid_dev, quarter), BF16),
        vm((n_dp, quarter, hid_dev), BF16), vm((n_dp, quarter, hid_dev), BF16),
        vm((n_dp, voc_dev, quarter), F32), vm((n_dp, voc_dev, quarter), BF16), vm((n_dp, voc_dev, quarter), BF16),
        vm((n_dp, hid_dev, quarter), F32), vm((n_dp, quarter, hid_dev), F32),
        vm((n_dp, voc_dev, quarter), BF16), vm((n_dp, voc_dev, quarter), BF16),
        vm((n_dp, hid_dev, quarter), BF16), vm((n_dp, hid_dev, quarter), BF16),
        vm((n_dp, quarter, hid_dev), BF16), vm((n_dp, quarter, hid_dev), BF16),
        vm((8, rows), F32), vm((8, 128), F32), vm((8, 128), F32),
        pltpu.SemaphoreType.DMA((N_GROUPS, chunks)), pltpu.SemaphoreType.DMA((N_GROUPS, chunks)),
        pltpu.SemaphoreType.DMA((3,)), pltpu.SemaphoreType.DMA((3,)),
        pltpu.SemaphoreType.DMA((3,)), pltpu.SemaphoreType.DMA((3,)),
    ]
    return kernel, scratch


def solution(mesh):
    n_seg, n_mp, n_dp = mesh.shape["segment"], mesh.shape["mp"], mesh.shape["dp"]

    def on_device(text_rows, durations, unit_targets, w_in, w_out, w_unit):
        micro, rows, width = text_rows.shape
        units = unit_targets.shape[1]
        hid_dev = w_in.shape[2]
        voc_dev = w_unit.shape[1]
        denom = float(micro * units * n_dp)
        kernel, scratch = make_kernel(
            n_seg, n_mp // 2, n_dp, micro // 2, 4, rows, width, hid_dev, voc_dev, units, denom
        )
        quarter = width // n_dp
        vmem = pl.BlockSpec(memory_space=pltpu.VMEM)
        loss, gin, gout, gun = pl.pallas_call(
            kernel,
            out_shape=(
                jax.ShapeDtypeStruct((1,), F32),
                jax.ShapeDtypeStruct((quarter, hid_dev), F32),
                jax.ShapeDtypeStruct((hid_dev, quarter), F32),
                jax.ShapeDtypeStruct((voc_dev, quarter), F32),
            ),
            in_specs=[pl.BlockSpec(memory_space=pl.ANY)] + [vmem] * 5,
            out_specs=(pl.BlockSpec(memory_space=pltpu.SMEM), vmem, vmem, vmem),
            scratch_shapes=scratch,
            compiler_params=pltpu.CompilerParams(
                collective_id=0, has_side_effects=True, vmem_limit_bytes=60 * 1024 * 1024
            ),
        )(
            text_rows, durations, unit_targets, w_in[0], w_out[0],
            jnp.transpose(w_unit),
        )
        return (loss, gin[None], gout[None], jnp.transpose(gun))

    placed = (
        P(None, "dp", None),
        P(None, "dp", None),
        P(None, "dp"),
        P("segment", None, "mp"),
        P("segment", "mp", None),
        P(None, ("segment", "mp")),
    )
    return jax.shard_map(
        on_device,
        mesh=mesh,
        in_specs=placed,
        out_specs=(
            P("dp"),
            P("segment", "dp", "mp"),
            P("segment", "mp", "dp"),
            P("dp", ("segment", "mp")),
        ),
        check_vma=False,
    )
```

time: 250 us -> 215 us (0.86)
  Pallas kernels: 243 us -> 208 us
    pallas_call x1, Pallas kernels: 243 us -> 208 us  [on_device(): pl.pallas_call(kernel, out_shape=(jax.ShapeDtypeStruct((1,), F32), jax.Sh...]
where the time goes in v2:
time: 215 us
  Pallas kernels  208 us (97%)
  local copies, waits for them, and re-layouts  3.65 us (2%)
  between operations  2.47 us (1%)
    pallas_call x1, Pallas kernels, on_device(): pl.pallas_call(kernel, out_shape=(jax.ShapeDtypeStruct((1,), F32), jax.Sh...  208 us

profile of v2, /device:TPU:1, one launch (start us, length us, event | category | flops | bytes accessed | tf_op | source)
XLA Modules:
  0.0 214.6 jit_solution(12761432799797170531)
XLA Ops:
  0.6 208.5 %shard_map.93 = (f32[1]{0:T(128)}, f32[256,512]{1,0:T(8,128)}, f32[512,256]{1,0:T(8,128)}, f32[160,256]{1,0:T(8,128)}) custom-call(bf16[4,128,1024]{2,1,0:T(8,128)(2,1)} %text.1, s32[4,1,128]{2,1,0:T(1,128)} %dur.1, s32[4,512]{1,0:T(4,128)} %tgt.1, bf16[1024,512]{1,0:T(8,128)(2,1)} %bitcast.6, bf16[512,1024]{1,0:T(8,128)(2,1)} %bitcast.7, ...), custom_call_target="tpu_custom_call" | custom-call | tf_op jit(solution)/shard_map/pallas_call | solution.py:576
  209.8 0.0 copy-start
  209.8 1.9 copy.15
  211.7 0.0 copy-done
  211.7 0.0 copy-start.1
  211.7 0.8 copy.16
  212.5 0.3 copy-done.1
  212.8 0.7 copy.17
Async XLA Ops:
  209.8 1.9 copy-start
  211.7 1.1 copy-start.1

commit v3 on v2

--- a/solution.py
+++ b/solution.py
@@ -98,12 +98,15 @@
         def drain(ref, sem):
             pltpu.make_async_copy(ref, ref, sem).wait()
 
-        def over(n, fn_of):
+        def span(start, stop, fn_of):
             def step(i, carry):
                 fn_of(i)
                 return carry
 
-            lax.fori_loop(0, n, step, 0)
+            lax.fori_loop(start, stop, step, 0)
+
+        def over(n, fn_of):
+            span(0, n, fn_of)
 
         def peers_z(fn_of):
             def step(i):
@@ -172,6 +175,11 @@
                 )
             )
 
+        def in_plane(src, dst, group, k):
+            peers_z(
+                lambda z2: put(src, dst, ssem.at[group, k], rsem.at[group, k], {"mp": 2 * z2 + c})
+            )
+
         def owned_sum(buf, k):
             total = buf[k, 0].astype(F32)
             for i in range(1, n_z):
@@ -239,8 +247,9 @@
                     )
 
                 over(n_seg - 1, send)
-
-        def staged(first, second):
+                in_plane(osh.at[k], fin.at[z, cds(k)], G_FINZ, k)
+
+        def staged(first, second, start, stop):
             def step(i):
                 @pl.when(i < chunks)
                 def _():
@@ -250,23 +259,12 @@
                 def _():
                     second(i - 1)
 
-            over(chunks + 1, step)
-
-        staged(forward, forward_end)
-        drain(wu_sib, rsem.at[G_LOSS, 1])
-        lvec[...] = jnp.zeros_like(lvec)
+            span(start, stop, step)
+
 
         def relay(k):
-            @pl.when(s < last)
-            def _():
-                drain(fin.at[z, cds(k)], rsem.at[G_FINY, k])
-
-            peers_z(
-                lambda z2: put(
-                    fin.at[z, cds(k)], fin.at[z, cds(k)], ssem.at[G_FINZ, k], rsem.at[G_FINZ, k],
-                    {"mp": 2 * z2 + c},
-                )
-            )
+            drain(fin.at[z, cds(k)], rsem.at[G_FINY, k])
+            in_plane(fin.at[z, cds(k)], fin.at[z, cds(k)], G_FINZ, k)
 
         def logits(k):
             for j in range(per):
@@ -318,7 +316,7 @@
             acc = norm_back(x, acc).astype(BF16)
             for i in range(n_z):
                 partd[i, mds(k), :] = acc[:, columns(i)]
-            scatter_z(partd, rsd, mds(k), k, G_NRS, k)
+            span(k * per, (k + 1) * per, lambda j: scatter_z(partd, rsd, cds(j), j, G_NRS, j))
 
         def norm_sum(k):
             drain(rsd.at[k, pl.ds(0, n_z - 1)], rsem.at[G_NRS, k])
@@ -329,21 +327,14 @@
                 put(ysend.at[k], yrecv.at[k, s], ssem.at[G_NY, k], rsem.at[G_NY, k], {"segment": last})
 
         def norm_end(k):
-            @pl.when(s == last)
-            def _():
-                drain(yrecv.at[k], rsem.at[G_NY, k])
-                total = ysend[k].astype(F32)
-                for i in range(n_seg - 1):
-                    total = total + yrecv[k, i].astype(F32)
-                grad = total.astype(BF16)
-                dsh[k] = grad
-                dxb[z, mds(k), :] = grad
-                peers_z(
-                    lambda z2: put(
-                        dsh.at[k], dxb.at[z, mds(k)], ssem.at[G_NAG, k], rsem.at[G_NAG, k],
-                        {"mp": 2 * z2 + c},
-                    )
-                )
+            drain(yrecv.at[k], rsem.at[G_NY, k])
+            total = ysend[k].astype(F32)
+            for i in range(n_seg - 1):
+                total = total + yrecv[k, i].astype(F32)
+            grad = total.astype(BF16)
+            dsh[k] = grad
+            dxb[z, cds(k), :] = grad
+            in_plane(dsh.at[k], dxb.at[z, cds(k)], G_NAG, k)
 
         def dp_send(xs, xr, g):
             def step(off):
@@ -384,27 +375,10 @@
             over(n_dp, unit_sum)
             dp_send(xs_u, xr_u, 0)
 
-        for k in range(per + 1):
-            relay(k)
-        logits(0)
-        for k in range(per + 1, chunks):
-            relay(k)
-        dlogits(0)
-        logits(1)
-        norm_sum(0)
-        dlogits(1)
-        norm_end(0)
-        norm_sum(1)
-        norm_end(1)
-
-        @pl.when(s < last)
-        def _():
-            unit_grad()
-
         def backward(k):
-            @pl.when((s == last) & (lax.rem(k, per) == 0))
-            def _():
-                drain(rsd.at[0, pl.ds(0, n_z - 1)], rsem.at[G_NAG, lax.div(k, per)])
+            @pl.when(s == last)
+            def _():
+                drain(rsd.at[0, pl.ds(0, n_z - 1)], rsem.at[G_NAG, k])
 
             @pl.when(s < last)
             def _():
@@ -439,10 +413,55 @@
                 peers_z(send)
                 send(z)
 
-        staged(backward, backward_end)
+        early = per + per // 2
+        staged(forward, forward_end, 0, early + 1)
+        drain(wu_sib, rsem.at[G_LOSS, 1])
+        lvec[...] = jnp.zeros_like(lvec)
 
         @pl.when(s == last)
         def _():
+            logits(0)
+
+        staged(forward, forward_end, early + 1, chunks + 1)
+
+        @pl.when(s < last)
+        def _():
+            over(early, relay)
+            logits(0)
+            span(early, chunks, relay)
+
+        dlogits(0)
+        logits(1)
+
+        @pl.when(s < last)
+        def _():
+            over(per - 1, norm_sum)
+            dlogits(1)
+            span(per - 1, chunks, norm_sum)
+            unit_grad()
+            staged(backward, backward_end, 0, chunks + 1)
+
+        @pl.when(s == last)
+        def _():
+            over(per - 1, norm_sum)
+            norm_end(0)
+            dlogits(1)
+            norm_sum(per - 1)
+            span(1, per, norm_end)
+
+            def first_half(i):
+                backward(i)
+                norm_sum(per + i)
+
+            over(per, first_half)
+
+            def second_half(i):
+                norm_end(per + i)
+                backward_end(i)
+
+            over(per, second_half)
+            span(per, chunks, backward)
+            span(per, chunks, backward_end)
             unit_grad()
 
         def grad_columns(q):
@@ -499,13 +518,17 @@
             drain(part_of, ssem.at[G_FRS, k])
             drain(part_of, ssem.at[G_FINZ, k])
 
+            drain(part_of, ssem.at[G_NRS, k])
+
             @pl.when(s < last)
             def _():
                 drain(rsf.at[0], ssem.at[G_FAG, k])
+                drain(ysend.at[k], ssem.at[G_NY, k])
 
             @pl.when(s == last)
             def _():
                 drain(osh.at[pl.ds(0, n_seg - 1)], ssem.at[G_FINY, k])
+                drain(part_of, ssem.at[G_NAG, k])
 
             @pl.when(s > 0)
             def _():
@@ -513,17 +536,7 @@
                 drain(rsf.at[0], ssem.at[G_BAG, k])
 
         def finish_micro(k):
-            part_of = rsd.at[0, pl.ds(0, n_z - 1)]
-            drain(part_of, ssem.at[G_NRS, k])
             drain(stb.at[k, pl.ds(0, n_peer - 1)], ssem.at[G_STAT, k])
-
-            @pl.when(s < last)
-            def _():
-                drain(ysend.at[k], ssem.at[G_NY, k])
-
-            @pl.when(s == last)
-            def _():
-                drain(part_of, ssem.at[G_NAG, k])
 
         over(chunks, finish)
         over(micros, finish_micro)
@@ -531,9 +544,7 @@
     vm = pltpu.VMEM
     lines = (n_z, all_rows, col)
     shard = (chunks, cut, col)
-    mshard = (micros, rows, col)
     scatter = (chunks, n_z, cut, col)
-    mscatter = (micros, n_z, rows, col)
     scratch = [
         vm((width, hid_dev), BF16), vm((hid_dev, width), BF16), vm((voc_dev, width), BF16),
         vm(lines, BF16), vm((all_rows, width), BF16), vm(lines, BF16),
@@ -541,8 +552,8 @@
         vm(lines, BF16), vm((all_rows, width), BF16),
         vm((micros, 2, voc_dev, rows), F32), vm((micros, 2, voc_dev, rows), F32),
         vm((micros, n_peer, 8, rows), F32), vm((2, micros, voc_dev, rows), BF16),
-        vm(lines, BF16), vm(mscatter, BF16), vm(mshard, BF16),
-        vm((micros, n_seg - 1, rows, col), BF16), vm(lines, BF16), vm(mshard, BF16),
+        vm(lines, BF16), vm(scatter, BF16), vm(shard, BF16),
+        vm((chunks, n_seg - 1, cut, col), BF16), vm(lines, BF16), vm(shard, BF16),
         vm((2, all_rows, hid_dev), BF16), vm(lines, BF16), vm(scatter, BF16), vm(shard, BF16),
         vm((n_dp, hid_dev, quarter), BF16), vm((n_dp, hid_dev, quarter), BF16),
         vm((n_dp, quarter, hid_dev), BF16), vm((n_dp, quarter, hid_dev), BF16),
@@ -569,7 +580,7 @@
         voc_dev = w_unit.shape[1]
         denom = float(micro * units * n_dp)
         kernel, scratch = make_kernel(
-            n_seg, n_mp // 2, n_dp, micro // 2, 4, rows, width, hid_dev, voc_dev, units, denom
+            n_seg, n_mp // 2, n_dp, micro // 2, 8, rows, width, hid_dev, voc_dev, units, denom
         )
         quarter = width // n_dp
         vmem = pl.BlockSpec(memory_space=pltpu.VMEM)

time: 215 us -> 200 us (0.930)
  Pallas kernels: 208 us -> 194 us
    pallas_call x1, Pallas kernels: 208 us -> 194 us  [on_device(): pl.pallas_call(kernel, out_shape=(jax.ShapeDtypeStruct((1,), F32), jax.Sh...]
where the time goes in v3:
time: 200 us
  Pallas kernels  194 us (97%)
  local copies, waits for them, and re-layouts  3.65 us (2%)
  between operations  2.47 us (1%)
    pallas_call x1, Pallas kernels, on_device(): pl.pallas_call(kernel, out_shape=(jax.ShapeDtypeStruct((1,), F32), jax.Sh...  194 us

profile of v3, /device:TPU:1, one launch (start us, length us, event | category | flops | bytes accessed | tf_op | source)
XLA Modules:
  0.0 200.0 jit_solution(10583392021480676439)
XLA Ops:
  0.6 193.9 %shard_map.93 = (f32[1]{0:T(128)}, f32[256,512]{1,0:T(8,128)}, f32[512,256]{1,0:T(8,128)}, f32[160,256]{1,0:T(8,128)}) custom-call(bf16[4,128,1024]{2,1,0:T(8,128)(2,1)} %text.1, s32[4,1,128]{2,1,0:T(1,128)} %dur.1, s32[4,512]{1,0:T(4,128)} %tgt.1, bf16[1024,512]{1,0:T(8,128)(2,1)} %bitcast.6, bf16[512,1024]{1,0:T(8,128)(2,1)} %bitcast.7, ...), custom_call_target="tpu_custom_call" | custom-call | tf_op jit(solution)/shard_map/pallas_call | solution.py:587
  195.3 0.0 copy-start
  195.3 1.9 copy.15
  197.2 0.0 copy-done
  197.2 0.0 copy-start.1
  197.2 0.8 copy.16
  198.0 0.3 copy-done.1
  198.2 0.7 copy.17
Async XLA Ops:
  195.3 1.9 copy-start
  197.2 1.1 copy-start.1

commit v4 on v3

--- a/solution.py
+++ b/solution.py
@@ -64,10 +64,10 @@
         xbuf, normed, part, rsf, osh, hid, slo,
         fin, fn, lg, cnt, stb, dlb, partd, rsd, ysend, yrecv, dxb, dsh,
         dpre, partb, rsb, bsh,
-        gs_sib, gr_sib, gi_sib, gir_sib, gu_f, gu_sib, gur_sib, go_f, gi_f,
-        xs_u, xr_u, xs_o, xr_o, xs_i, xr_i,
+        normed_sib, hidden_all, dx_all, dpre_sib, gu_f, gu_sib, gur_sib, gi_f,
+        xs_u, xr_u, xs_i, xr_i,
         lvec, lown, lrcv,
-        ssem, rsem, sib_s, sib_r, dp_s, dp_r,
+        ssem, rsem, sib_s, sib_r, dp_s, dp_r, ex_s, ex_r,
     ):
         s = lax.axis_index("segment")
         mp = lax.axis_index("mp")
@@ -197,7 +197,8 @@
 
             x = whole(xbuf, cds(k)).astype(F32)
             n = (x * row_scale(x)).astype(BF16)
-            normed[cds(k), :] = n
+            for i in range(n_z):
+                normed[i, cds(k), :] = n[:, columns(i)]
 
             value, slope = gelu_parts(nn(n, w_in[...]))
             h0 = value.astype(BF16)
@@ -389,6 +390,17 @@
             dpre[0, cds(k), :] = p0
             p1 = (nt(g, wo_sib[...]) * slo[1, cds(k), :]).astype(BF16)
             dpre[1, cds(k), :] = p1
+            put(dpre.at[1, cds(k)], dpre_sib.at[cds(k)], ex_s.at[3], ex_r.at[3], {"mp": sib})
+
+            def share(off):
+                other = lax.rem(2 * d + c + off, 2 * n_dp)
+                d2 = lax.div(other, 2)
+                put(
+                    dxb.at[pl.ds(d2 * blocks, blocks), cds(k)], dx_all.at[2 * d + c, :, cds(k)],
+                    ex_s.at[2], ex_r.at[2], {"dp": d2, "mp": 2 * z + lax.rem(other, 2)},
+                )
+
+            span(1, 2 * n_dp, share)
 
             @pl.when(s > 0)
             def _():
@@ -413,6 +425,19 @@
                 peers_z(send)
                 send(z)
 
+        def share_hidden():
+            put(normed, normed_sib, ex_s.at[0], ex_r.at[0], {"mp": sib})
+
+            def step(off):
+                other = lax.rem(2 * d + c + off, 2 * n_dp)
+                c2 = lax.rem(other, 2)
+                put(
+                    hid.at[lax.rem(c + c2, 2)], hidden_all.at[2 * d + c],
+                    ex_s.at[1], ex_r.at[1], {"dp": lax.div(other, 2), "mp": 2 * z + c2},
+                )
+
+            span(1, 2 * n_dp, step)
+
         early = per + per // 2
         staged(forward, forward_end, 0, early + 1)
         drain(wu_sib, rsem.at[G_LOSS, 1])
@@ -426,6 +451,7 @@
 
         @pl.when(s < last)
         def _():
+            share_hidden()
             over(early, relay)
             logits(0)
             span(early, chunks, relay)
@@ -449,6 +475,8 @@
             norm_sum(per - 1)
             span(1, per, norm_end)
 
+            share_hidden()
+
             def first_half(i):
                 backward(i)
                 norm_sum(per + i)
@@ -464,54 +492,50 @@
             span(per, chunks, backward_end)
             unit_grad()
 
-        def grad_columns(q):
-            return jnp.concatenate([dxb[q * blocks + i] for i in range(blocks)], axis=-1)
-
-        for q in range(n_dp):
-            gs_sib[q] = tn(hid[1], grad_columns(q)).astype(BF16)
-        put(gs_sib, gr_sib, sib_s.at[1], sib_r.at[1], {"mp": sib})
-        for q in range(n_dp):
-            go_f[q] = tn(hid[0], grad_columns(q))
-        for q in range(n_dp):
-            gi_sib[q] = tn(normed[:, q * quarter : (q + 1) * quarter], dpre[1]).astype(BF16)
-        put(gi_sib, gir_sib, sib_s.at[2], sib_r.at[2], {"mp": sib})
-        drain(gr_sib, sib_r.at[1])
-
-        def out_sum(q):
-            total = go_f[q] + gr_sib[q].astype(F32)
-            go_f[q] = total
-            xs_o[q] = total.astype(BF16)
-
-        over(n_dp, out_sum)
-        dp_send(xs_o, xr_o, 1)
-        for q in range(n_dp):
-            gi_f[q] = tn(normed[:, q * quarter : (q + 1) * quarter], dpre[0])
-        drain(gir_sib, sib_r.at[2])
-
-        def in_sum(q):
-            total = gi_f[q] + gir_sib[q].astype(F32)
-            gi_f[q] = total
-            xs_i[q] = total.astype(BF16)
-
-        over(n_dp, in_sum)
-        dp_send(xs_i, xr_i, 2)
+        drain(dpre_sib, ex_r.at[3])
+        drain(normed_sib, ex_r.at[0])
+
+        def in_quarter(q):
+            own = jnp.concatenate([normed[q * blocks + i] for i in range(blocks)], axis=-1)
+            other = jnp.concatenate([normed_sib[q * blocks + i] for i in range(blocks)], axis=-1)
+            return tn(own, dpre[0]) + tn(other, dpre_sib[...])
+
+        def in_send(off):
+            d2 = lax.rem(d + off + 1, n_dp)
+            xs_i[d2] = in_quarter(d2).astype(BF16)
+            put(xs_i.at[d2], xr_i.at[d], dp_s.at[1], dp_r.at[1], {"dp": d2})
+
+        over(n_dp - 1, in_send)
+        gi_f[...] = in_quarter(d)
+
+        drain(hidden_all.at[pl.ds(0, 2 * n_dp - 1)], ex_r.at[1])
+        drain(dx_all.at[pl.ds(0, 2 * n_dp - 1)], ex_r.at[2])
+        own_dx = jnp.concatenate([dxb[d * blocks + i] for i in range(blocks)], axis=-1)
+        gout_o[...] = tn(hid[0], own_dx)
+
+        def out_term(off):
+            other = lax.rem(2 * d + c + off, 2 * n_dp)
+            got = jnp.concatenate([dx_all[other, i] for i in range(blocks)], axis=-1)
+            gout_o[...] += tn(hidden_all[other], got)
+
+        span(1, 2 * n_dp, out_term)
 
         dp_out(gu_f[d], xr_u, 0, gun_o)
         drain(lrcv, rsem.at[G_LOSS, 0])
         loss_o[0] = jnp.max(lown[...] + lrcv[...]) * (1.0 / denom)
-        dp_out(go_f[d], xr_o, 1, gout_o)
-        dp_out(gi_f[d], xr_i, 2, gin_o)
+        dp_out(gi_f[...], xr_i, 1, gin_o)
 
         drain(w_in, ssem.at[G_SIBW, 0])
         drain(w_out, ssem.at[G_SIBW, 1])
         drain(w_unit, ssem.at[G_LOSS, 1])
         drain(lown, ssem.at[G_LOSS, 0])
         drain(gu_sib, sib_s.at[0])
-        drain(gs_sib, sib_s.at[1])
-        drain(gi_sib, sib_s.at[2])
         drain(xs_u.at[pl.ds(0, n_dp - 1)], dp_s.at[0])
-        drain(xs_o.at[pl.ds(0, n_dp - 1)], dp_s.at[1])
-        drain(xs_i.at[pl.ds(0, n_dp - 1)], dp_s.at[2])
+        drain(xs_i.at[pl.ds(0, n_dp - 1)], dp_s.at[1])
+        drain(normed, ex_s.at[0])
+        drain(hidden_all.at[pl.ds(0, 2 * n_dp - 1)], ex_s.at[1])
+        drain(dx_all.at[pl.ds(0, 2 * n_dp - 1)], ex_s.at[2])
+        drain(dpre_sib, ex_s.at[3])
 
         def finish(k):
             part_of = rsf.at[0, pl.ds(0, n_z - 1)]
@@ -547,7 +571,7 @@
     scatter = (chunks, n_z, cut, col)
     scratch = [
         vm((width, hid_dev), BF16), vm((hid_dev, width), BF16), vm((voc_dev, width), BF16),
-        vm(lines, BF16), vm((all_rows, width), BF16), vm(lines, BF16),
+        vm(lines, BF16), vm(lines, BF16), vm(lines, BF16),
         vm(scatter, BF16), vm(shard, BF16), vm((2, all_rows, hid_dev), BF16), vm((2, all_rows, hid_dev), F32),
         vm(lines, BF16), vm((all_rows, width), BF16),
         vm((micros, 2, voc_dev, rows), F32), vm((micros, 2, voc_dev, rows), F32),
@@ -555,17 +579,17 @@
         vm(lines, BF16), vm(scatter, BF16), vm(shard, BF16),
         vm((chunks, n_seg - 1, cut, col), BF16), vm(lines, BF16), vm(shard, BF16),
         vm((2, all_rows, hid_dev), BF16), vm(lines, BF16), vm(scatter, BF16), vm(shard, BF16),
-        vm((n_dp, hid_dev, quarter), BF16), vm((n_dp, hid_dev, quarter), BF16),
-        vm((n_dp, quarter, hid_dev), BF16), vm((n_dp, quarter, hid_dev), BF16),
+        vm(lines, BF16), vm((2 * n_dp, all_rows, hid_dev), BF16),
+        vm((2 * n_dp, n_z // n_dp, all_rows, col), BF16), vm((all_rows, hid_dev), BF16),
         vm((n_dp, voc_dev, quarter), F32), vm((n_dp, voc_dev, quarter), BF16), vm((n_dp, voc_dev, quarter), BF16),
-        vm((n_dp, hid_dev, quarter), F32), vm((n_dp, quarter, hid_dev), F32),
+        vm((quarter, hid_dev), F32),
         vm((n_dp, voc_dev, quarter), BF16), vm((n_dp, voc_dev, quarter), BF16),
-        vm((n_dp, hid_dev, quarter), BF16), vm((n_dp, hid_dev, quarter), BF16),
         vm((n_dp, quarter, hid_dev), BF16), vm((n_dp, quarter, hid_dev), BF16),
         vm((8, rows), F32), vm((8, 128), F32), vm((8, 128), F32),
         pltpu.SemaphoreType.DMA((N_GROUPS, chunks)), pltpu.SemaphoreType.DMA((N_GROUPS, chunks)),
-        pltpu.SemaphoreType.DMA((3,)), pltpu.SemaphoreType.DMA((3,)),
-        pltpu.SemaphoreType.DMA((3,)), pltpu.SemaphoreType.DMA((3,)),
+        pltpu.SemaphoreType.DMA((1,)), pltpu.SemaphoreType.DMA((1,)),
+        pltpu.SemaphoreType.DMA((2,)), pltpu.SemaphoreType.DMA((2,)),
+        pltpu.SemaphoreType.DMA((4,)), pltpu.SemaphoreType.DMA((4,)),
     ]
     return kernel, scratch
 

time: 200 us -> 190 us (0.950)
  Pallas kernels: 194 us -> 183 us
    pallas_call x1, Pallas kernels: 194 us -> 183 us  [on_device(): pl.pallas_call(kernel, out_shape=(jax.ShapeDtypeStruct((1,), F32), jax.Sh...]
where the time goes in v4:
time: 190 us; the launch traced here: 189 us
  Pallas kernels  183 us (96%)
  local copies, waits for them, and re-layouts  3.65 us (2%)
  between operations  2.47 us (1%)
    pallas_call x1, Pallas kernels, on_device(): pl.pallas_call(kernel, out_shape=(jax.ShapeDtypeStruct((1,), F32), jax.Sh...  183 us

profile of v4, /device:TPU:1, one launch (start us, length us, event | category | flops | bytes accessed | tf_op | source)
XLA Modules:
  0.0 189.5 jit_solution(5288721743244665180)
XLA Ops:
  0.6 183.4 %shard_map.93 = (f32[1]{0:T(128)}, f32[256,512]{1,0:T(8,128)}, f32[512,256]{1,0:T(8,128)}, f32[160,256]{1,0:T(8,128)}) custom-call(bf16[4,128,1024]{2,1,0:T(8,128)(2,1)} %text.1, s32[4,1,128]{2,1,0:T(1,128)} %dur.1, s32[4,512]{1,0:T(4,128)} %tgt.1, bf16[1024,512]{1,0:T(8,128)(2,1)} %bitcast.6, bf16[512,1024]{1,0:T(8,128)(2,1)} %bitcast.7, ...), custom_call_target="tpu_custom_call" | custom-call | tf_op jit(solution)/shard_map/pallas_call | solution.py:611
  184.7 0.0 copy-start
  184.7 1.9 %copy.15 = f32[1,256,512]{2,1,0:T(8,128)} copy(f32[1,256,512]{2,1,0:T(8,128)} %bitcast.9) | data formatting | bytes 1048576
  186.6 0.0 copy-done
  186.6 0.0 copy-start.1
  186.6 0.8 copy.16
  187.4 0.3 copy-done.1
  187.7 0.7 copy.17
Async XLA Ops:
  184.7 1.9 %copy-start = (f32[512,256]{1,0:T(8,128)S(1)}, f32[512,256]{1,0:T(8,128)}, u32[]{:S(2)}) copy-start(f32[512,256]{1,0:T(8,128)} %get-tuple-element.10) | copy-start | bytes 1572868
  186.6 1.1 copy-start.1

commit v5 on v4

--- a/solution.py
+++ b/solution.py
@@ -77,6 +77,7 @@
         sib = 2 * z + (1 - c)
         me = s * n_z + z
         last = n_seg - 1
+        hub = n_seg - 2
 
         def cds(k):
             return pl.ds(pl.multiple_of(k * cut, cut), cut)
@@ -284,7 +285,7 @@
             hit = jnp.sum(cnt[k, 0] * a, axis=0, keepdims=True) + jnp.sum(
                 cnt[k, 1] * b, axis=0, keepdims=True
             )
-            sub = lax.broadcasted_iota(jnp.int32, (8, rows), 0)
+            sub = lax.broadcasted_iota(jnp.int32, (4, rows), 0)
             stb[k, me] = jnp.where(sub == 0, peak, jnp.where(sub == 1, total, hit))
 
             def send(off):
@@ -323,19 +324,26 @@
             drain(rsd.at[k, pl.ds(0, n_z - 1)], rsem.at[G_NRS, k])
             ysend[k] = owned_sum(rsd, k).astype(BF16)
 
-            @pl.when(s < last)
-            def _():
-                put(ysend.at[k], yrecv.at[k, s], ssem.at[G_NY, k], rsem.at[G_NY, k], {"segment": last})
+            @pl.when(s != hub)
+            def _():
+                slot = jnp.minimum(s, hub)
+                put(ysend.at[k], yrecv.at[k, slot], ssem.at[G_NY, k], rsem.at[G_NY, k], {"segment": hub})
 
         def norm_end(k):
             drain(yrecv.at[k], rsem.at[G_NY, k])
             total = ysend[k].astype(F32)
             for i in range(n_seg - 1):
                 total = total + yrecv[k, i].astype(F32)
-            grad = total.astype(BF16)
-            dsh[k] = grad
-            dxb[z, cds(k), :] = grad
-            in_plane(dsh.at[k], dxb.at[z, cds(k)], G_NAG, k)
+            dsh[k] = total.astype(BF16)
+
+            def send(z2):
+                put(
+                    dsh.at[k], dxb.at[z, cds(k)], ssem.at[G_NAG, k], rsem.at[G_NAG, k],
+                    {"segment": last, "mp": 2 * z2 + c},
+                )
+
+            peers_z(send)
+            send(z)
 
         def dp_send(xs, xr, g):
             def step(off):
@@ -379,7 +387,7 @@
         def backward(k):
             @pl.when(s == last)
             def _():
-                drain(rsd.at[0, pl.ds(0, n_z - 1)], rsem.at[G_NAG, k])
+                drain(dxb.at[:, cds(k)], rsem.at[G_NAG, k])
 
             @pl.when(s < last)
             def _():
@@ -390,6 +398,15 @@
             dpre[0, cds(k), :] = p0
             p1 = (nt(g, wo_sib[...]) * slo[1, cds(k), :]).astype(BF16)
             dpre[1, cds(k), :] = p1
+
+            @pl.when(s > 0)
+            def _():
+                x = whole(xbuf, cds(k)).astype(F32)
+                acc = norm_back(x, nt(p0, w_in[...]) + nt(p1, wi_sib[...])).astype(BF16)
+                for i in range(n_z):
+                    partb[i, cds(k), :] = acc[:, columns(i)]
+                scatter_z(partb, rsb, cds(k), k, G_BRS, k)
+
             put(dpre.at[1, cds(k)], dpre_sib.at[cds(k)], ex_s.at[3], ex_r.at[3], {"mp": sib})
 
             def share(off):
@@ -402,14 +419,6 @@
 
             span(1, 2 * n_dp, share)
 
-            @pl.when(s > 0)
-            def _():
-                x = whole(xbuf, cds(k)).astype(F32)
-                acc = norm_back(x, nt(p0, w_in[...]) + nt(p1, wi_sib[...])).astype(BF16)
-                for i in range(n_z):
-                    partb[i, cds(k), :] = acc[:, columns(i)]
-                scatter_z(partb, rsb, cds(k), k, G_BRS, k)
-
         def backward_end(k):
             @pl.when(s > 0)
             def _():
@@ -451,30 +460,44 @@
 
         @pl.when(s < last)
         def _():
-            share_hidden()
             over(early, relay)
             logits(0)
             span(early, chunks, relay)
+            share_hidden()
 
         dlogits(0)
         logits(1)
 
+        over(per - 1, norm_sum)
+
+        @pl.when(s == hub)
+        def _():
+            norm_end(0)
+
+        dlogits(1)
+        norm_sum(per - 1)
+
+        @pl.when(s == hub)
+        def _():
+            span(1, per, norm_end)
+
         @pl.when(s < last)
         def _():
-            over(per - 1, norm_sum)
-            dlogits(1)
-            span(per - 1, chunks, norm_sum)
+            def late(i):
+                @pl.when(i < chunks)
+                def _():
+                    norm_sum(i)
+
+                @pl.when((s == hub) & (i >= per + 2))
+                def _():
+                    norm_end(i - 2)
+
+            span(per, chunks + 2, late)
             unit_grad()
             staged(backward, backward_end, 0, chunks + 1)
 
         @pl.when(s == last)
         def _():
-            over(per - 1, norm_sum)
-            norm_end(0)
-            dlogits(1)
-            norm_sum(per - 1)
-            span(1, per, norm_end)
-
             share_hidden()
 
             def first_half(i):
@@ -482,12 +505,7 @@
                 norm_sum(per + i)
 
             over(per, first_half)
-
-            def second_half(i):
-                norm_end(per + i)
-                backward_end(i)
-
-            over(per, second_half)
+            over(per, backward_end)
             span(per, chunks, backward)
             span(per, chunks, backward_end)
             unit_grad()
@@ -544,15 +562,21 @@
 
             drain(part_of, ssem.at[G_NRS, k])
 
+            @pl.when(s != hub)
+            def _():
+                drain(ysend.at[k], ssem.at[G_NY, k])
+
+            @pl.when(s == hub)
+            def _():
+                drain(rsf.at[0], ssem.at[G_NAG, k])
+
             @pl.when(s < last)
             def _():
                 drain(rsf.at[0], ssem.at[G_FAG, k])
-                drain(ysend.at[k], ssem.at[G_NY, k])
 
             @pl.when(s == last)
             def _():
                 drain(osh.at[pl.ds(0, n_seg - 1)], ssem.at[G_FINY, k])
-                drain(part_of, ssem.at[G_NAG, k])
 
             @pl.when(s > 0)
             def _():
@@ -575,7 +599,7 @@
         vm(scatter, BF16), vm(shard, BF16), vm((2, all_rows, hid_dev), BF16), vm((2, all_rows, hid_dev), F32),
         vm(lines, BF16), vm((all_rows, width), BF16),
         vm((micros, 2, voc_dev, rows), F32), vm((micros, 2, voc_dev, rows), F32),
-        vm((micros, n_peer, 8, rows), F32), vm((2, micros, voc_dev, rows), BF16),
+        vm((micros, n_peer, 4, rows), F32), vm((2, micros, voc_dev, rows), BF16),
         vm(lines, BF16), vm(scatter, BF16), vm(shard, BF16),
         vm((chunks, n_seg - 1, cut, col), BF16), vm(lines, BF16), vm(shard, BF16),
         vm((2, all_rows, hid_dev), BF16), vm(lines, BF16), vm(scatter, BF16), vm(shard, BF16),

time: 190 us -> 184 us (0.968)
  Pallas kernels: 183 us -> 177 us
    pallas_call x1, Pallas kernels: 183 us -> 177 us  [on_device(): pl.pallas_call(kernel, out_shape=(jax.ShapeDtypeStruct((1,), F32), jax.Sh...]
where the time goes in v5:
time: 184 us
  Pallas kernels  177 us (96%)
  local copies, waits for them, and re-layouts  3.65 us (2%)
  between operations  2.47 us (1%)
    pallas_call x1, Pallas kernels, on_device(): pl.pallas_call(kernel, out_shape=(jax.ShapeDtypeStruct((1,), F32), jax.Sh...  177 us

profile of v5, /device:TPU:1, one launch (start us, length us, event | category | flops | bytes accessed | tf_op | source)
XLA Modules:
  0.0 183.5 jit_solution(8512993337954851013)
XLA Ops:
  0.6 177.4 %shard_map.93 = (f32[1]{0:T(128)}, f32[256,512]{1,0:T(8,128)}, f32[512,256]{1,0:T(8,128)}, f32[160,256]{1,0:T(8,128)}) custom-call(bf16[4,128,1024]{2,1,0:T(8,128)(2,1)} %text.1, s32[4,1,128]{2,1,0:T(1,128)} %dur.1, s32[4,512]{1,0:T(4,128)} %tgt.1, bf16[1024,512]{1,0:T(8,128)(2,1)} %bitcast.6, bf16[512,1024]{1,0:T(8,128)(2,1)} %bitcast.7, ...), custom_call_target="tpu_custom_call" | custom-call | tf_op jit(solution)/shard_map/pallas_call | solution.py:635
  178.7 0.0 copy-start
  178.7 1.9 %copy.15 = f32[1,256,512]{2,1,0:T(8,128)} copy(f32[1,256,512]{2,1,0:T(8,128)} %bitcast.9) | data formatting | bytes 1048576
  180.6 0.0 copy-done
  180.6 0.0 copy-start.1
  180.7 0.8 copy.16
  181.4 0.3 copy-done.1
  181.7 0.7 copy.17
Async XLA Ops:
  178.7 1.9 %copy-start = (f32[512,256]{1,0:T(8,128)S(1)}, f32[512,256]{1,0:T(8,128)}, u32[]{:S(2)}) copy-start(f32[512,256]{1,0:T(8,128)} %get-tuple-element.10) | copy-start | bytes 1572868
  180.6 1.1 copy-start.1

commit v6 on v5

--- a/solution.py
+++ b/solution.py
@@ -58,9 +58,9 @@
     blocks = n_z // n_dp
 
     def kernel(
-        text, dur, tgt, w_in, w_out, w_unit,
+        text, dur, tgt, w_in_h, w_out_h, w_unit_h,
         loss_o, gin_o, gout_o, gun_o,
-        wi_sib, wo_sib, wu_sib,
+        w_in, w_out, w_unit, wi_sib, wo_sib, wu_sib,
         xbuf, normed, part, rsf, osh, hid, slo,
         fin, fn, lg, cnt, stb, dlb, partd, rsd, ysend, yrecv, dxb, dsh,
         dpre, partb, rsb, bsh,
@@ -77,7 +77,7 @@
         sib = 2 * z + (1 - c)
         me = s * n_z + z
         last = n_seg - 1
-        hub = n_seg - 2
+        hub = 0
 
         def cds(k):
             return pl.ds(pl.multiple_of(k * cut, cut), cut)
@@ -142,6 +142,10 @@
                     ).start()
 
             over(chunks, load)
+
+        pltpu.make_async_copy(w_in_h, w_in, rsem.at[G_SIBW, 2]).start()
+        pltpu.make_async_copy(w_out_h, w_out, rsem.at[G_SIBW, 3]).start()
+        pltpu.make_async_copy(w_unit_h, w_unit, rsem.at[G_LOSS, 2]).start()
 
         def count(k):
             lengths = dur[micros * c + k].astype(F32)
@@ -163,9 +167,9 @@
         over(micros, count)
         pl.semaphore_wait(barrier, n_z - 1 + n_seg - 1 + n_dp - 1 + 1)
 
-        put(w_in, wi_sib, ssem.at[G_SIBW, 0], rsem.at[G_SIBW, 0], {"mp": sib})
-        put(w_out, wo_sib, ssem.at[G_SIBW, 1], rsem.at[G_SIBW, 1], {"mp": sib})
-        put(w_unit, wu_sib, ssem.at[G_LOSS, 1], rsem.at[G_LOSS, 1], {"mp": sib})
+        put(w_in_h, wi_sib, ssem.at[G_SIBW, 0], rsem.at[G_SIBW, 0], {"mp": sib})
+        put(w_out_h, wo_sib, ssem.at[G_SIBW, 1], rsem.at[G_SIBW, 1], {"mp": sib})
+        put(w_unit_h, wu_sib, ssem.at[G_LOSS, 1], rsem.at[G_LOSS, 1], {"mp": sib})
 
         def scatter_z(buf, got, where, slot, group, k):
             own = got.at[slot, z]
@@ -201,6 +205,11 @@
             for i in range(n_z):
                 normed[i, cds(k), :] = n[:, columns(i)]
 
+            @pl.when(k == 0)
+            def _():
+                drain(w_in, rsem.at[G_SIBW, 2])
+                drain(w_out, rsem.at[G_SIBW, 3])
+
             value, slope = gelu_parts(nn(n, w_in[...]))
             h0 = value.astype(BF16)
             hid[0, cds(k), :] = h0
@@ -210,12 +219,16 @@
             @pl.when(k == 0)
             def _():
                 drain(wi_sib, rsem.at[G_SIBW, 0])
-                drain(wo_sib, rsem.at[G_SIBW, 1])
 
             value, slope = gelu_parts(nn(n, wi_sib[...]))
             h1 = value.astype(BF16)
             hid[1, cds(k), :] = h1
             slo[1, cds(k), :] = slope
+
+            @pl.when(k == 0)
+            def _():
+                drain(wo_sib, rsem.at[G_SIBW, 1])
+
             acc = (acc + nn(h1, wo_sib[...])).astype(BF16)
             for i in range(n_z):
                 part[i, cds(k), :] = acc[:, columns(i)]
@@ -288,8 +301,9 @@
             sub = lax.broadcasted_iota(jnp.int32, (4, rows), 0)
             stb[k, me] = jnp.where(sub == 0, peak, jnp.where(sub == 1, total, hit))
 
-            def send(off):
-                other = lax.rem(me + off + 1, n_peer)
+            def send(i):
+                side = 1 - 2 * lax.rem(i, 2)
+                other = lax.rem(me + n_peer // 2 + side * lax.div(i + 1, 2), n_peer)
                 put(
                     stb.at[k, me], stb.at[k, me], ssem.at[G_STAT, k], rsem.at[G_STAT, k],
                     {"segment": lax.div(other, n_z), "mp": 2 * lax.rem(other, n_z) + c},
@@ -326,8 +340,7 @@
 
             @pl.when(s != hub)
             def _():
-                slot = jnp.minimum(s, hub)
-                put(ysend.at[k], yrecv.at[k, slot], ssem.at[G_NY, k], rsem.at[G_NY, k], {"segment": hub})
+                put(ysend.at[k], yrecv.at[k, s - 1], ssem.at[G_NY, k], rsem.at[G_NY, k], {"segment": hub})
 
         def norm_end(k):
             drain(yrecv.at[k], rsem.at[G_NY, k])
@@ -447,9 +460,10 @@
 
             span(1, 2 * n_dp, step)
 
-        early = per + per // 2
+        early = per + 1
         staged(forward, forward_end, 0, early + 1)
         drain(wu_sib, rsem.at[G_LOSS, 1])
+        drain(w_unit, rsem.at[G_LOSS, 2])
         lvec[...] = jnp.zeros_like(lvec)
 
         @pl.when(s == last)
@@ -518,8 +532,9 @@
             other = jnp.concatenate([normed_sib[q * blocks + i] for i in range(blocks)], axis=-1)
             return tn(own, dpre[0]) + tn(other, dpre_sib[...])
 
-        def in_send(off):
-            d2 = lax.rem(d + off + 1, n_dp)
+        def in_send(i):
+            side = 1 - 2 * lax.rem(i, 2)
+            d2 = lax.rem(d + n_dp // 2 + side * lax.div(i + 1, 2), n_dp)
             xs_i[d2] = in_quarter(d2).astype(BF16)
             put(xs_i.at[d2], xr_i.at[d], dp_s.at[1], dp_r.at[1], {"dp": d2})
 
@@ -594,6 +609,7 @@
     shard = (chunks, cut, col)
     scatter = (chunks, n_z, cut, col)
     scratch = [
+        vm((width, hid_dev), BF16), vm((hid_dev, width), BF16), vm((voc_dev, width), BF16),
         vm((width, hid_dev), BF16), vm((hid_dev, width), BF16), vm((voc_dev, width), BF16),
         vm(lines, BF16), vm(lines, BF16), vm(lines, BF16),
         vm(scatter, BF16), vm(shard, BF16), vm((2, all_rows, hid_dev), BF16), vm((2, all_rows, hid_dev), F32),
@@ -632,6 +648,7 @@
         )
         quarter = width // n_dp
         vmem = pl.BlockSpec(memory_space=pltpu.VMEM)
+        hbm = pl.BlockSpec(memory_space=pl.ANY)
         loss, gin, gout, gun = pl.pallas_call(
             kernel,
             out_shape=(
@@ -640,7 +657,7 @@
                 jax.ShapeDtypeStruct((hid_dev, quarter), F32),
                 jax.ShapeDtypeStruct((voc_dev, quarter), F32),
             ),
-            in_specs=[pl.BlockSpec(memory_space=pl.ANY)] + [vmem] * 5,
+            in_specs=[hbm, vmem, vmem, hbm, hbm, hbm],
             out_specs=(pl.BlockSpec(memory_space=pltpu.SMEM), vmem, vmem, vmem),
             scratch_shapes=scratch,
             compiler_params=pltpu.CompilerParams(

time: 184 us -> 183 us (level)
  no operation moved by 1% of the time
where the time goes in v6:
time: 183 us
  Pallas kernels  177 us (97%)
  local copies, waits for them, and re-layouts  3.65 us (2%)
  between operations  2.47 us (1%)
    pallas_call x1, Pallas kernels, on_device(): pl.pallas_call(kernel, out_shape=(jax.ShapeDtypeStruct((1,), F32), jax.Sh...  177 us

profile of v6, /device:TPU:1, one launch (start us, length us, event | category | flops | bytes accessed | tf_op | source)
XLA Modules:
  0.0 182.6 jit_solution(12358711760415990065)
XLA Ops:
  0.6 176.5 %shard_map.93 = (f32[1]{0:T(128)}, f32[256,512]{1,0:T(8,128)}, f32[512,256]{1,0:T(8,128)}, f32[160,256]{1,0:T(8,128)}) custom-call(bf16[4,128,1024]{2,1,0:T(8,128)(2,1)} %text.1, s32[4,1,128]{2,1,0:T(1,128)} %dur.1, s32[4,512]{1,0:T(4,128)} %tgt.1, bf16[1024,512]{1,0:T(8,128)(2,1)} %bitcast.6, bf16[512,1024]{1,0:T(8,128)(2,1)} %bitcast.7, ...), custom_call_target="tpu_custom_call" | custom-call | tf_op jit(solution)/shard_map/pallas_call | solution.py:652
  177.8 0.0 copy-start
  177.9 1.9 %copy.15 = f32[1,256,512]{2,1,0:T(8,128)} copy(f32[1,256,512]{2,1,0:T(8,128)} %bitcast.9) | data formatting | bytes 1048576
  179.8 0.0 copy-done
  179.8 0.0 copy-start.1
  179.8 0.8 copy.16
  180.6 0.3 copy-done.1
  180.8 0.7 copy.17
Async XLA Ops:
  177.8 1.9 %copy-start = (f32[512,256]{1,0:T(8,128)S(1)}, f32[512,256]{1,0:T(8,128)}, u32[]{:S(2)}) copy-start(f32[512,256]{1,0:T(8,128)} %get-tuple-element.10) | copy-start | bytes 1572868
  179.8 1.1 copy-start.1

commit v7 on v6

--- a/solution.py
+++ b/solution.py
@@ -59,12 +59,12 @@
 
     def kernel(
         text, dur, tgt, w_in_h, w_out_h, w_unit_h,
-        loss_o, gin_o, gout_o, gun_o,
+        loss_o, gin_o, gi_f, gout_o, gun_o,
         w_in, w_out, w_unit, wi_sib, wo_sib, wu_sib,
         xbuf, normed, part, rsf, osh, hid, slo,
         fin, fn, lg, cnt, stb, dlb, partd, rsd, ysend, yrecv, dxb, dsh,
         dpre, partb, rsb, bsh,
-        normed_sib, hidden_all, dx_all, dpre_sib, gu_f, gu_sib, gur_sib, gi_f,
+        normed_sib, hidden_all, dx_all, dpre_sib, gu_f, gu_sib, gur_sib,
         xs_u, xr_u, xs_i, xr_i,
         lvec, lown, lrcv,
         ssem, rsem, sib_s, sib_r, dp_s, dp_r, ex_s, ex_r,
@@ -369,7 +369,8 @@
             drain(xr.at[pl.ds(0, n_dp - 1)], dp_r.at[g])
             total = own
             for off in range(1, n_dp):
-                total = total + xr[lax.rem(d + off, n_dp)].astype(F32)
+                term = xr[lax.rem(d + off, n_dp)].astype(F32)
+                total = term if total is None else total + term
             out[...] = total
 
         def unit_grad():
@@ -556,7 +557,7 @@
         dp_out(gu_f[d], xr_u, 0, gun_o)
         drain(lrcv, rsem.at[G_LOSS, 0])
         loss_o[0] = jnp.max(lown[...] + lrcv[...]) * (1.0 / denom)
-        dp_out(gi_f[...], xr_i, 1, gin_o)
+        dp_out(None, xr_i, 1, gin_o)
 
         drain(w_in, ssem.at[G_SIBW, 0])
         drain(w_out, ssem.at[G_SIBW, 1])
@@ -622,7 +623,6 @@
         vm(lines, BF16), vm((2 * n_dp, all_rows, hid_dev), BF16),
         vm((2 * n_dp, n_z // n_dp, all_rows, col), BF16), vm((all_rows, hid_dev), BF16),
         vm((n_dp, voc_dev, quarter), F32), vm((n_dp, voc_dev, quarter), BF16), vm((n_dp, voc_dev, quarter), BF16),
-        vm((quarter, hid_dev), F32),
         vm((n_dp, voc_dev, quarter), BF16), vm((n_dp, voc_dev, quarter), BF16),
         vm((n_dp, quarter, hid_dev), BF16), vm((n_dp, quarter, hid_dev), BF16),
         vm((8, rows), F32), vm((8, 128), F32), vm((8, 128), F32),
@@ -649,16 +649,17 @@
         quarter = width // n_dp
         vmem = pl.BlockSpec(memory_space=pltpu.VMEM)
         hbm = pl.BlockSpec(memory_space=pl.ANY)
-        loss, gin, gout, gun = pl.pallas_call(
+        loss, gin, gin_own, gout, gun = pl.pallas_call(
             kernel,
             out_shape=(
                 jax.ShapeDtypeStruct((1,), F32),
+                jax.ShapeDtypeStruct((quarter, hid_dev), F32),
                 jax.ShapeDtypeStruct((quarter, hid_dev), F32),
                 jax.ShapeDtypeStruct((hid_dev, quarter), F32),
                 jax.ShapeDtypeStruct((voc_dev, quarter), F32),
             ),
             in_specs=[hbm, vmem, vmem, hbm, hbm, hbm],
-            out_specs=(pl.BlockSpec(memory_space=pltpu.SMEM), vmem, vmem, vmem),
+            out_specs=(pl.BlockSpec(memory_space=pltpu.SMEM), vmem, vmem, vmem, vmem),
             scratch_shapes=scratch,
             compiler_params=pltpu.CompilerParams(
                 collective_id=0, has_side_effects=True, vmem_limit_bytes=60 * 1024 * 1024
@@ -667,7 +668,7 @@
             text_rows, durations, unit_targets, w_in[0], w_out[0],
             jnp.transpose(w_unit),
         )
-        return (loss, gin[None], gout[None], jnp.transpose(gun))
+        return (loss, (gin + gin_own)[None], gout[None], jnp.transpose(gun))
 
     placed = (
         P(None, "dp", None),

time: 183 us -> 183 us (level)
  other arithmetic: 0 us -> 2.13 us
  local copies, waits for them, and re-layouts: 3.65 us -> 1.7 us
    broadcast_in_dim x0 -> x1, other arithmetic: none -> 2.13 us  [on_device(): return (loss, (gin + gin_own)[None], gout[None], jnp.transpose(gun))]
    unnamed x7 -> x6, local copies, waits for them, and re-layouts: 3.65 us -> 1.7 us
where the time goes in v7:
time: 183 us
  Pallas kernels  176 us (96%)
  between operations  2.41 us (1%)
  other arithmetic  2.13 us (1%)
    pallas_call x1, Pallas kernels, on_device(): pl.pallas_call(kernel, out_shape=(jax.ShapeDtypeStruct((1,), F32), jax.Sh...  176 us

profile of v7, /device:TPU:1, one launch (start us, length us, event | category | flops | bytes accessed | tf_op | source)
XLA Modules:
  0.0 182.6 jit_solution(8068454944458251418)
XLA Ops:
  0.6 176.4 %shard_map.93 = (f32[1]{0:T(128)}, f32[256,512]{1,0:T(8,128)}, f32[256,512]{1,0:T(8,128)}, f32[512,256]{1,0:T(8,128)}, f32[160,256]{1,0:T(8,128)}) custom-call(bf16[4,128,1024]{2,1,0:T(8,128)(2,1)} %text.1, s32[4,1,128]{2,1,0:T(1,128)} %dur.1, s32[4,512]{1,0:T(4,128)} %tgt.1, bf16[1024,512]{1,0:T(8,128)(2,1)} %bitcast.7, bf16[512,1024]{1,0:T(8,128)(2,1)} %bitcast.8, ...), custom_call_target="tpu_custom_call" | custom-call | tf_op jit(solution)/shard_map/pallas_call | solution.py:652
  177.0 0.0 copy-start
  177.0 2.1 %add_bitcast_fusion = f32[1,256,512]{2,1,0:T(8,128)} fusion(f32[256,512]{1,0:T(8,128)} %get-tuple-element.10, f32[256,512]{1,0:T(8,128)} %get-tuple-element.11), kind=kLoop, calls=%fused_computation | loop fusion | flops 131072 | bytes 1572864 | tf_op jit(solution)/shard_map/broadcast_in_dim | solution.py:671
  179.7 0.0 copy-done
  179.8 0.0 copy-start.1
  179.8 0.8 copy.14
  180.6 0.2 copy-done.1
  180.8 0.7 copy.15
Async XLA Ops:
  177.0 2.8 %copy-start = (f32[512,256]{1,0:T(8,128)S(1)}, f32[512,256]{1,0:T(8,128)}, u32[]{:S(2)}) copy-start(f32[512,256]{1,0:T(8,128)} %get-tuple-element.12) | copy-start | bytes 1572868
  179.8 1.0 copy-start.1
